TPU v7x, 128 devices: a whole 4x4x4 slice. The times are simulated.
128 devices in a mesh: wave: 32 (over x, z, core), dof: 4 (over y).
Axes of the slice: x: 4, y: 4, z: 4, core: 2. Of those that a mesh axis runs over, the one named last changes fastest.
Arguments:
- green: bfloat16 [2, 2048, 512, 512], P(None, 'wave', None, 'dof'), may hold values from -0.25 to 0.25
- rough: float32 [2, 2048, 512], P(None, 'wave'), may hold values from -6 to 6
- axle_pos: int32 [128, 32], replicated, may hold values from 0 to 2047
- axle_load: float32 [128, 32], replicated, may hold values from 0.5 to 1.5
- rows: int32 [1024, 16], replicated, may hold values from 0 to 2047
- counts: int32 [1024], replicated, may hold values from 1 to 16, as said below
- coupling: bfloat16 [1024, 512], P(None, 'dof'), may hold values from -0.25 to 0.25
Outputs:
- response: float32 [1024, 128], P('dof', 'wave')
Inputs may be any that keep to these rules, and one draw needn't show every extreme that they name: Building b uses its first counts[b] stations; some building uses all 16.
All inputs are finite; a program needn't handle non-finite values.
Results may differ from a plain program's by a relative error of at most 0.005.
Values may be sent and summed in bfloat16 or wider, within the bound.
A program may use at most 320 MiB of HBM per device.

v0:
```python
import math

import jax
import jax.numpy as jnp
from jax import lax
from jax.sharding import PartitionSpec as P

K = 2048


def make_table():
    stations = jnp.arange(K, dtype=jnp.int32)
    product = stations[:, None] * stations[None, :] % K
    angle = product.astype(jnp.float32) * (2.0 * math.pi / K)
    scale = 1.0 / math.sqrt(K)
    table = jnp.stack([jnp.cos(angle) * scale, -jnp.sin(angle) * scale], axis=2)
    return table.reshape(K, 2 * K).astype(jnp.bfloat16)


def building_terms(field, coupling_part, occupancy, counts):
    flat = field.reshape(field.shape[0], field.shape[1] * field.shape[2])
    gathered = jnp.dot(
        occupancy.astype(jnp.float32),
        flat,
        precision=lax.Precision.HIGHEST,
        preferred_element_type=jnp.float32,
    )
    gathered = gathered.reshape(occupancy.shape[0], field.shape[1], field.shape[2])
    summed = jnp.einsum(
        "bi,bic->bc", coupling_part.astype(jnp.float32), gathered, precision=lax.Precision.HIGHEST
    )
    return summed / counts.astype(jnp.float32)[:, None]


def arrange_owned(partial_sum, building_count, case_count):
    wave_size = lax.axis_size("wave")
    dof_size = lax.axis_size("dof")
    arranged = partial_sum.reshape(
        dof_size, building_count // dof_size, wave_size, case_count // wave_size
    )
    arranged = jnp.transpose(arranged, (2, 0, 1, 3))
    return arranged.reshape(wave_size * building_count, case_count // wave_size)


def body(green, rough, axle_pos, axle_load, rows, counts, coupling):
    wave_count = green.shape[1]
    case_count = axle_pos.shape[0]
    building_count = rows.shape[0]
    slot_count = rows.shape[1]
    waves = lax.axis_index("wave") * wave_count + jnp.arange(wave_count, dtype=jnp.int32)
    product = waves[:, None, None] * axle_pos[None, :, :] % K
    angle = product.astype(jnp.float32) * (2.0 * math.pi / K)
    norm_axle = 1.0 / math.sqrt(axle_pos.shape[1])
    phase_re = jnp.sum(axle_load[None] * jnp.cos(angle), axis=2) * norm_axle
    phase_im = -jnp.sum(axle_load[None] * jnp.sin(angle), axis=2) * norm_axle
    force_re = (
        rough[0][:, :, None] * phase_re[:, None, :] - rough[1][:, :, None] * phase_im[:, None, :]
    )
    force_im = (
        rough[0][:, :, None] * phase_im[:, None, :] + rough[1][:, :, None] * phase_re[:, None, :]
    )
    force = jnp.concatenate([force_re, force_im], axis=2).astype(jnp.bfloat16)
    prod_real = jnp.einsum("mji,mjc->mic", green[0], force, preferred_element_type=jnp.float32)
    prod_imag = jnp.einsum("mji,mjc->mic", green[1], force, preferred_element_type=jnp.float32)
    spec_re = prod_real[:, :, :case_count] - prod_imag[:, :, case_count:]
    spec_im = prod_real[:, :, case_count:] + prod_imag[:, :, :case_count]
    spectra = jnp.stack([spec_re, spec_im], axis=1).astype(jnp.bfloat16)
    slots = (jnp.arange(slot_count, dtype=jnp.int32)[None, :] < counts[:, None]).astype(jnp.float32)
    building_ids = jnp.broadcast_to(
        jnp.arange(building_count, dtype=jnp.int32)[:, None], (building_count, slot_count)
    )
    occupancy = (
        jnp.zeros((building_count, K), jnp.float32)
        .at[building_ids, rows]
        .add(slots)
        .astype(jnp.bfloat16)
    )
    table = make_table()
    group_in = lax.all_to_all(spectra, "wave", split_axis=2, concat_axis=0, tiled=True)
    first_len = group_in.shape[2]
    second_len = group_in.shape[3]
    flat = group_in.reshape(group_in.shape[0] * 2, first_len * second_len)
    field = jnp.dot(table, flat, preferred_element_type=jnp.float32)
    field = field.reshape(table.shape[0], first_len, second_len)
    dof_sub = field.shape[1]
    coupling_part = lax.dynamic_slice_in_dim(coupling, lax.axis_index("wave") * dof_sub, dof_sub, 1)
    partial_sum = building_terms(field, coupling_part, occupancy, counts)
    arranged = arrange_owned(partial_sum, building_count, case_count)
    return lax.psum_scatter(arranged, ("wave", "dof"), scatter_dimension=0, tiled=True)


def solution(mesh):
    in_specs = (
        P(None, "wave", None, "dof"),
        P(None, "wave", None),
        P(),
        P(),
        P(),
        P(),
        P(None, "dof"),
    )
    out_specs = P("dof", "wave")
    return jax.shard_map(body, mesh=mesh, in_specs=in_specs, out_specs=out_specs, check_vma=False)
```

profile of v0, /device:TPU:1, one launch (start us, length us, event | category | flops | bytes accessed | tf_op | source)
XLA Modules:
  0.0 1020.7 jit_solution(613872975529454945)
XLA Ops:
  6.5 1.0 slice_bitcast_fusion.1
  7.5 5.7 multiply_reduce_fusion.2
  13.2 7.4 subtract_convert_fusion
  20.6 13.1 %fusion.19 = f32[64,128,256]{1,2,0:T(8,128)} fusion(bf16[2,64,512,128]{3,2,1,0:T(8,128)(2,1)} %param.7, bf16[64,512,128]{1,2,0:T(8,128)(2,1)} %get-tuple-element.10, bf16[64,512,128]{1,2,0:T(8,128)(2,1)} %get-tuple-element.9), kind=kOutput, calls=%fused_computation.32 | convolution fusion | flops 2181038080 | bytes 33554432 | tf_op jit(solution)/shard_map/mji,mjc->mic/dot_general | solution.py:63
  33.7 13.1 %fusion.22 = f32[64,128,256]{1,2,0:T(8,128)} fusion(bf16[2,64,512,128]{3,2,1,0:T(8,128)(2,1)} %param.7, bf16[64,512,128]{1,2,0:T(8,128)(2,1)} %get-tuple-element.10, bf16[64,512,128]{1,2,0:T(8,128)(2,1)} %get-tuple-element.9), kind=kOutput, calls=%fused_computation.33 | convolution fusion | flops 2181038080 | bytes 33554432 | tf_op jit(solution)/shard_map/mji,mjc->mic/dot_general | solution.py:64
  46.8 6.8 fusion.25
  53.6 2.3 pad_maximum_fusion.4
  55.9 6.6 copy.33
  62.5 9.5 all-to-all-start
  72.0 0.2 reduce-scatter.4.cloned.1.call-start
  72.2 67.7 %multiply_convert_fusion = (bf16[2048,2048,1]{1,0,2:T(8,128)(2,1)S(1)}, bf16[2048,2048,1]{1,0,2:T(8,128)(2,1)S(1)}) fusion(), kind=kLoop, calls=%fused_computation.11 | loop fusion | flops 79691776 | bytes 16777216 | tf_op jit(solution)/shard_map/convert.7
  139.9 6.8 pad_maximum_fusion
  146.7 41.7 %copy.32 = bf16[2048,2048,2]{0,2,1:T(2,128)(2,1)} copy(bf16[2048,2048,2]{1,0,2:T(8,128)(2,1)} %pad_maximum_fusion) | data formatting | bytes 33554432 | tf_op jit(solution)/shard_map/stack | solution.py:16
  188.5 0.0 copy-start.2
  188.5 0.0 copy-start.5
  188.5 0.0 copy-start.4
  188.5 0.0 copy-start.3
  188.5 24.9 %convert_element_type.45 = bf16[2048,4096]{0,1:T(8,128)(2,1)} reshape(bf16[2048,2048,2]{0,2,1:T(2,128)(2,1)} %copy.32) | data formatting | bytes 33554432 | tf_op jit(solution)/shard_map/convert_element_type | solution.py:17
  213.4 0.0 copy-done.2
  213.4 0.0 copy-done.5
  213.4 0.1 multiply_reduce_fusion.3
  213.5 0.0 copy-done.4
  213.5 0.1 and_reduce_fusion
  213.7 0.2 copy.31
  213.9 0.2 reshape.136
  214.1 0.0 copy-done.3
  214.1 0.2 fusion.30
  214.3 0.2 reshape.138
  214.5 89.8 %scatter_custom_fusion = f32[2097152]{0:T(1024)} fusion(s32[16384]{0:T(1024)S(1)} %reshape.136, f32[16384]{0:T(1024)S(1)} %reshape.138, f32[]{:T(128)} %constant.24.clone.1), kind=kCustom, calls=%fused_computation.30 | custom fusion | flops 16384 | bytes 8388612
  304.3 0.0 copy-start.1
  304.3 5.1 convert_element_type.48
  309.4 7.3 reshape.135
  316.7 0.0 copy-done.1
  316.7 0.1 dynamic-slice_convert_fusion
  316.9 0.2 copy.47
  317.1 0.0 all-to-all-done
  317.1 6.2 copy.35
  323.2 0.0 copy-start
  323.2 12.0 %fusion.12 = f32[2048,512]{1,0:T(8,128)S(1)} fusion(bf16[2048,4096]{0,1:T(8,128)(2,1)} %convert_element_type.45, bf16[512,8,4,128]{3,2,1,0:T(4,128)(2,1)S(1)} %bitcast.44), kind=kOutput, calls=%fused_computation.22 | convolution fusion | flops 8589934592 | bytes 25165824 | tf_op jit(solution)/shard_map/dot_general | solution.py:83
  335.3 0.0 copy-done
  335.3 6.7 fusion.34
  342.0 0.3 multiply_reduce_fusion
  342.3 0.1 broadcast_divide_fusion
  342.3 0.2 reshape.129
  342.6 8.4 copy.45
  351.0 0.0 reduce-scatter.4.cloned.1.call-update
  351.0 661.3 %reduce-scatter.4.cloned.1.call-done = f32[256,4]{1,0:T(8,128)} async-done(((f32[32768,4]{1,0:T(8,128)}), f32[256,4]{1,0:T(8,128)}) %reduce-scatter.4.cloned.1.call-update) | async-done | bytes 4112
  1012.3 1.6 copy.44
  (6 shorter events, 0.0 us)
Async XLA Ops:
  62.5 254.6 %all-to-all-start = ((bf16[64,2,128,128]{3,0,1,2:T(8,128)(2,1)}), bf16[64,2,128,128]{3,0,1,2:T(8,128)(2,1)}, u32[]{:S(2)}, u32[]{:S(2)}) async-start(bf16[64,2,128,128]{3,0,1,2:T(8,128)(2,1)} %copy.33), calls=%async_computation | async-start | bytes 8388608 | tf_op jit(solution)/shard_map/all_to_all | solution.py:79
  72.0 940.3 %reduce-scatter.4.cloned.1.call-start = ((), (), s32[]{:S(2)}) async-start(), calls=%async_computation.2 | async-start | bytes 16908288
  188.5 25.0 %copy-start.2 = (s32[1024,16]{0,1:T(8,128)S(1)}, s32[1024,16]{0,1:T(8,128)}, u32[]{:S(2)}) copy-start(s32[1024,16]{0,1:T(8,128)} %param.11) | copy-start | bytes 196612
  188.5 25.0 %copy-start.5 = (s32[2]{0:T(128)S(1)}, s32[2]{0:T(128)}, u32[]{:S(2)}) copy-start(s32[2]{0:T(128)} %constant.50) | copy-start | bytes 28
  188.5 25.1 %copy-start.4 = (s32[2]{0:T(128)S(1)}, s32[2]{0:T(128)}, u32[]{:S(2)}) copy-start(s32[2]{0:T(128)} %constant.53) | copy-start | bytes 28
  188.5 25.6 %copy-start.3 = (s32[1024]{0:T(1024)S(1)}, s32[1024]{0:T(1024)}, u32[]{:S(2)}) copy-start(s32[1024]{0:T(1024)} %param.12) | copy-start | bytes 12292
  304.3 12.4 %copy-start.1 = (bf16[1024,128]{1,0:T(8,128)(2,1)S(1)}, bf16[1024,128]{1,0:T(8,128)(2,1)}, u32[]{:S(2)}) copy-start(bf16[1024,128]{1,0:T(8,128)(2,1)} %param.13) | copy-start | bytes 786436
  323.2 12.1 %copy-start = (bf16[1024,2048]{1,0:T(8,128)(2,1)S(1)}, bf16[1024,2048]{1,0:T(8,128)(2,1)}, u32[]{:S(2)}) copy-start(bf16[1024,2048]{1,0:T(8,128)(2,1)} %reshape.135) | copy-start | bytes 12582916
Sparse Core Ops, SparseCore 0:
  351.1 661.1 reduce-scatter.3
where the time goes:
time: 1030 us; the launch traced here: 1020 us
  waiting for transfers between devices  661 us (64%)
  other arithmetic  192 us (19%)
  local copies, waits for them, and re-layouts  98.7 us (10%)
  matrix products  44.9 us (4%)
  between operations  13.6 us (1%)
    unnamed x2, waiting for transfers between devices  661 us
    unnamed x5, other arithmetic  90.1 us
    another operation x2, other arithmetic  75.1 us
    another operation x1, local copies, waits for them, and re-layouts, make_table(): table = jnp.stack([jnp.cos(angle) * scale, -jnp.sin(angle) * scale], axis=2)  41.7 us
    convert_element_type x1, local copies, waits for them, and re-layouts, make_table(): return table.reshape(K, 2 * K).astype(jnp.bfloat16)  24.9 us
  transfers between devices with their start and end apart: 2, of which 1 were waited for; matrix products, arithmetic and copies ran while one was open for 24% of the time, Pallas kernels for 0%

commit v1 on v0

v1 whole, which is shorter than its diff:
```python
import math

import jax
import jax.numpy as jnp
from jax import lax
from jax.sharding import PartitionSpec as P

K = 2048


def split_bf16(x):
    hi = x.astype(jnp.bfloat16)
    lo = (x - hi.astype(jnp.float32)).astype(jnp.bfloat16)
    return hi, lo


def body(green, rough, axle_pos, axle_load, rows, counts, coupling):
    wave_count = green.shape[1]
    case_count = axle_pos.shape[0]
    building_count = rows.shape[0]
    slot_count = rows.shape[1]
    dof_size = lax.axis_size("dof")
    own_buildings = building_count // dof_size
    waves = lax.axis_index("wave") * wave_count + jnp.arange(wave_count, dtype=jnp.int32)

    product = waves[:, None, None] * axle_pos[None, :, :] % K
    angle = product.astype(jnp.float32) * (2.0 * math.pi / K)
    norm_axle = 1.0 / math.sqrt(axle_pos.shape[1])
    phase_re = jnp.sum(axle_load[None] * jnp.cos(angle), axis=2) * norm_axle
    phase_im = -jnp.sum(axle_load[None] * jnp.sin(angle), axis=2) * norm_axle

    re_hi, re_lo = split_bf16(rough[0])
    im_hi, im_lo = split_bf16(rough[1])
    lhs = jnp.stack([re_hi, re_lo, im_hi, im_lo], axis=1)
    prod = jnp.einsum("mkj,gmji->gmki", lhs, green, preferred_element_type=jnp.float32)
    gre_rre = prod[0, :, 0] + prod[0, :, 1]
    gre_rim = prod[0, :, 2] + prod[0, :, 3]
    gim_rre = prod[1, :, 0] + prod[1, :, 1]
    gim_rim = prod[1, :, 2] + prod[1, :, 3]
    h_cat = jnp.concatenate([gre_rre - gim_rim, gre_rim + gim_rre], axis=0)

    h_hi, h_lo = split_bf16(h_cat)
    rhs = jnp.concatenate([h_hi, h_lo], axis=0)
    both = jnp.einsum("bi,ni->bn", coupling, rhs, preferred_element_type=jnp.float32)
    v_part = both[:, : 2 * wave_count] + both[:, 2 * wave_count :]
    v_own = lax.psum_scatter(v_part, "dof", scatter_dimension=0, tiled=True)
    v_re = v_own[:, :wave_count]
    v_im = v_own[:, wave_count:]

    first = lax.axis_index("dof") * own_buildings
    rows_own = lax.dynamic_slice_in_dim(rows, first, own_buildings, 0)
    counts_own = lax.dynamic_slice_in_dim(counts, first, own_buildings, 0)
    used = (jnp.arange(slot_count, dtype=jnp.int32)[None, :] < counts_own[:, None]).astype(jnp.float32)
    station_prod = rows_own[:, :, None] * waves[None, None, :] % K
    station_angle = station_prod.astype(jnp.float32) * (2.0 * math.pi / K)
    scale = 1.0 / math.sqrt(K)
    t_re = (jnp.cos(station_angle) * scale).astype(jnp.bfloat16).astype(jnp.float32)
    t_im = (-jnp.sin(station_angle) * scale).astype(jnp.bfloat16).astype(jnp.float32)
    w_re = jnp.sum(used[:, :, None] * t_re, axis=1)
    w_im = jnp.sum(used[:, :, None] * t_im, axis=1)

    a_part = w_re * v_re + w_im * v_im
    b_part = w_im * v_re - w_re * v_im
    ab = jnp.concatenate([a_part, b_part], axis=1)
    phase_cat = jnp.concatenate([phase_re, phase_im], axis=0)
    partial = jnp.dot(
        phase_cat.T, ab.T, precision=lax.Precision.HIGHEST, preferred_element_type=jnp.float32
    )
    summed = lax.psum_scatter(partial, "wave", scatter_dimension=0, tiled=True)
    return summed.T / counts_own.astype(jnp.float32)[:, None]


def solution(mesh):
    in_specs = (
        P(None, "wave", None, "dof"),
        P(None, "wave", None),
        P(),
        P(),
        P(),
        P(),
        P(None, "dof"),
    )
    out_specs = P("dof", "wave")
    return jax.shard_map(body, mesh=mesh, in_specs=in_specs, out_specs=out_specs, check_vma=False)
```

time: 1030 us -> 153 us (0.15)
  waiting for transfers between devices: 661 us -> 113 us
  other arithmetic: 192 us -> 13.7 us
  local copies, waits for them, and re-layouts: 98.7 us -> 2.62 us
  matrix products: 44.9 us -> 8.37 us
    unnamed x2 -> x3, waiting for transfers between devices: 661 us -> 101 us
    another operation x5 -> x0, other arithmetic: 91 us -> none
    unnamed x5 -> x0, other arithmetic: 90.1 us -> none
    another operation x2 -> x0, local copies, waits for them, and re-layouts: 48.3 us -> none  [the longest x1 41.7 us: make_table(): table = jnp.stack([jnp.cos(angle) * scale, -jnp.sin(angle) * scale], axis=2)]
    dot_general x4 -> x3, matrix products: 44.9 us -> 8.37 us  [the longest x1 7.12 us: body(): jnp.einsum('mkj,gmji->gmki', lhs, green, preferred_element_type=jnp.float32)]
    convert_element_type x3 -> x1, local copies, waits for them, and re-layouts: 32.4 us -> 0.27 us  [split_bf16(): hi = x.astype(jnp.bfloat16)]
    reduce_scatter x0 -> x1, waiting for transfers between devices: none -> 12.1 us  [body(): v_own = lax.psum_scatter(v_part, 'dof', scatter_dimension=0, tiled=True)]
  transfers between devices with their start and end apart: 2 -> 2, of which waited for: 1 -> 2; matrix products, arithmetic and copies ran while one was open for 24% -> 8% of each run, Pallas kernels for 0% -> 0%
where the time goes in v1:
time: 153 us; the launch traced here: 152 us
  waiting for transfers between devices  113 us (74%)
  between operations  14.2 us (9%)
  other arithmetic  13.7 us (9%)
  matrix products  8.37 us (5%)
  local copies, waits for them, and re-layouts  2.62 us (2%)
    unnamed x3, waiting for transfers between devices  101 us
    reduce_scatter x1, waiting for transfers between devices, body(): v_own = lax.psum_scatter(v_part, 'dof', scatter_dimension=0, tiled=True)  12.1 us
    dot_general x1, matrix products, body(): jnp.einsum('mkj,gmji->gmki', lhs, green, preferred_element_type=jnp.float32)  7.12 us
    reduce_sum x1, other arithmetic, body(): phase_re = jnp.sum(axle_load[None] * jnp.cos(angle), axis=2) * norm_axle  4.91 us
    reduce_sum x1, other arithmetic, body(): w_im = jnp.sum(used[:, :, None] * t_im, axis=1)  4.49 us
  transfers between devices with their start and end apart: 2, of which 2 were waited for; matrix products, arithmetic and copies ran while one was open for 8% of the time, Pallas kernels for 0%

profile of v1, /device:TPU:1, one launch (start us, length us, event | category | flops | bytes accessed | tf_op | source)
XLA Modules:
  0.0 152.4 jit_solution(2851922674232542858)
XLA Ops:
  6.5 0.0 copy-start
  6.5 0.0 copy-start.3
  6.5 0.0 copy-start.2
  6.5 0.0 copy-start.1
  6.5 0.0 reduce-scatter.2.cloned.1.call-start
  6.6 1.0 fusion.38
  7.6 0.3 fusion.21
  7.9 0.3 subtract_convert_fusion
  8.2 7.1 %fusion.2 = f32[2,64,4,128]{3,2,0,1:T(4,128)S(1)} fusion(bf16[2,64,512,128]{3,2,1,0:T(8,128)(2,1)} %param.7, bf16[64,1,512]{2,1,0:T(2,128)(2,1)S(1)} %get-tuple-element.20, bf16[64,1,512]{2,1,0:T(2,128)(2,1)S(1)} %get-tuple-element.23, bf16[64,1,512]{2,1,0:T(2,128)(2,1)S(1)} %get-tuple-element.21, bf16[64,1,512]{2,1,0:T(2,128)(2,1)S(1)} %get-tuple-element.22), kind=kOutput, calls=%fused_computation.13 | convolution fusion | flops 68157440 | bytes 17301504 | tf_op jit(solution)/shard_map/mkj,gmji->gmki/dot_general | solution.py:35
  15.3 0.2 fusion.37
  15.5 0.0 copy-done
  15.5 0.3 convolution_bitcast_fusion
  15.8 0.8 slice_add_fusion
  16.7 0.0 reduce-scatter.2.cloned.1.call-update
  16.7 0.0 all-reduce.3.cloned.1.call-start
  16.8 0.8 fusion.36
  17.5 0.7 constant_dynamic-slice_fusion
  18.2 0.0 copy-done.2
  18.3 0.0 copy-done.1
  18.3 4.9 %multiply_reduce_fusion.3 = (f32[64,128]{1,0:T(8,128)S(1)}, f32[64,128]{1,0:T(8,128)S(1)}) fusion(s32[128,32]{0,1:T(8,128)S(1)} %copy-done.1, s32[64]{0:T(128)S(1)} %iota_add_fusion, f32[128,32]{0,1:T(8,128)S(1)} %copy-done.2), kind=kLoop, calls=%fused_computation.25 | loop fusion | flops 4702208 | bytes 98560 | tf_op jit(solution)/shard_map/reduce_sum | solution.py:29
  23.2 4.5 %multiply_reduce_fusion = (f32[256,64]{0,1:T(8,128)S(1)}, f32[256,64]{0,1:T(8,128)S(1)}) fusion(s32[64]{0:T(128)S(1)} %iota_add_fusion, s32[256,16]{0,1:T(8,128)S(1)} %constant_dynamic-slice_fusion, f32[256,16]{0,1:T(8,128)S(1)} %fusion.31), kind=kLoop, calls=%fused_computation.20 | loop fusion | flops 6520832 | bytes 164096 | tf_op jit(solution)/shard_map/reduce_sum | solution.py:60
  27.7 12.1 %reduce-scatter.2.cloned.1.call-done = f32[256,128]{0,1:T(8,128)} async-done(((f32[1024,128]{0,1:T(8,128)}), f32[256,128]{0,1:T(8,128)}) %reduce-scatter.2.cloned.1.call-update) | async-done | bytes 131088 | tf_op jit(solution)/shard_map/reduce_scatter | solution.py:46
  39.8 0.9 multiply_add_fusion
  40.7 1.0 fusion.17
  41.7 0.0 all-reduce.3.cloned.1.call-update
  41.7 0.0 copy-done.3
  41.7 0.6 dynamic-slice
  42.9 101.3 %all-reduce.3.cloned.1.call-done = f32[128,256]{1,0:T(8,128)} async-done(((f32[128,256]{1,0:T(8,128)}), f32[128,256]{1,0:T(8,128)}) %all-reduce.3.cloned.1.call-update) | async-done | bytes 131088
  144.3 1.3 fusion.32
  (6 shorter events, 0.0 us)
Async XLA Ops:
  6.5 9.0 %copy-start = (bf16[1024,128]{1,0:T(8,128)(2,1)S(1)}, bf16[1024,128]{1,0:T(8,128)(2,1)}, u32[]{:S(2)}) copy-start(bf16[1024,128]{1,0:T(8,128)(2,1)} %param.13) | copy-start | bytes 786436
  6.5 35.2 %copy-start.3 = (u32[128]{0:T(128)S(1)}, u32[128]{0:T(128)}, u32[]{:S(2)}) copy-start(u32[128]{0:T(128)} %constant.50) | copy-start | bytes 1540
  6.5 11.7 %copy-start.2 = (f32[128,32]{0,1:T(8,128)S(1)}, f32[128,32]{0,1:T(8,128)}, u32[]{:S(2)}) copy-start(f32[128,32]{0,1:T(8,128)} %param.10) | copy-start | bytes 49156
  6.5 11.7 %copy-start.1 = (s32[128,32]{0,1:T(8,128)S(1)}, s32[128,32]{0,1:T(8,128)}, u32[]{:S(2)}) copy-start(s32[128,32]{0,1:T(8,128)} %param.9) | copy-start | bytes 49156
  6.5 33.3 %reduce-scatter.2.cloned.1.call-start = ((), (), s32[]{:S(2)}) async-start(), calls=%async_computation.1 | async-start | bytes 655360 | tf_op jit(solution)/shard_map/reduce_scatter | solution.py:46
  16.7 127.6 %all-reduce.3.cloned.1.call-start = ((), (), s32[]{:S(2)}) async-start(), calls=%async_computation.2 | async-start | bytes 262144
Sparse Core Ops, SparseCore 0:
  16.8 22.9 reduce-scatter.1
  43.0 101.1 all-reduce.2

commit v2 on v1

--- a/solution.py
+++ b/solution.py
@@ -3,6 +3,8 @@
 import jax
 import jax.numpy as jnp
 from jax import lax
+from jax.experimental import pallas as pl
+from jax.experimental.pallas import tpu as pltpu
 from jax.sharding import PartitionSpec as P
 
 K = 2048
@@ -12,6 +14,52 @@
     hi = x.astype(jnp.bfloat16)
     lo = (x - hi.astype(jnp.float32)).astype(jnp.bfloat16)
     return hi, lo
+
+
+def scatter_sum(x, axis, collective_id):
+    n = x.shape[0]
+    block = x.shape[1:]
+    mesh_id = pl.DeviceIdType.MESH
+
+    def kernel(x_ref, out_ref, recv, send_sems, recv_sems):
+        me = lax.axis_index(axis)
+        barrier = pltpu.get_barrier_semaphore()
+        for k in range(1, n):
+            peer = lax.rem(me + k, n)
+            pl.semaphore_signal(barrier, inc=1, device_id={axis: peer}, device_id_type=mesh_id)
+        pl.semaphore_wait(barrier, n - 1)
+        copies = []
+        for k in range(1, n):
+            peer = lax.rem(me + k, n)
+            copy = pltpu.make_async_remote_copy(
+                src_ref=x_ref.at[peer],
+                dst_ref=recv.at[k - 1],
+                send_sem=send_sems.at[k - 1],
+                recv_sem=recv_sems.at[k - 1],
+                device_id={axis: peer},
+                device_id_type=mesh_id,
+            )
+            copy.start()
+            copies.append(copy)
+        for copy in copies:
+            copy.wait()
+        total = x_ref[me]
+        for k in range(n - 1):
+            total = total + recv[k]
+        out_ref[...] = total
+
+    return pl.pallas_call(
+        kernel,
+        out_shape=jax.ShapeDtypeStruct(block, x.dtype),
+        in_specs=[pl.BlockSpec(memory_space=pltpu.VMEM)],
+        out_specs=pl.BlockSpec(memory_space=pltpu.VMEM),
+        scratch_shapes=[
+            pltpu.VMEM((n - 1,) + block, x.dtype),
+            pltpu.SemaphoreType.DMA((n - 1,)),
+            pltpu.SemaphoreType.DMA((n - 1,)),
+        ],
+        compiler_params=pltpu.CompilerParams(collective_id=collective_id, has_side_effects=True),
+    )(x)
 
 
 def body(green, rough, axle_pos, axle_load, rows, counts, coupling):
@@ -43,7 +91,7 @@
     rhs = jnp.concatenate([h_hi, h_lo], axis=0)
     both = jnp.einsum("bi,ni->bn", coupling, rhs, preferred_element_type=jnp.float32)
     v_part = both[:, : 2 * wave_count] + both[:, 2 * wave_count :]
-    v_own = lax.psum_scatter(v_part, "dof", scatter_dimension=0, tiled=True)
+    v_own = scatter_sum(v_part.reshape(dof_size, own_buildings, 2 * wave_count), "dof", 0)
     v_re = v_own[:, :wave_count]
     v_im = v_own[:, wave_count:]
 
@@ -66,7 +114,8 @@
     partial = jnp.dot(
         phase_cat.T, ab.T, precision=lax.Precision.HIGHEST, preferred_element_type=jnp.float32
     )
-    summed = lax.psum_scatter(partial, "wave", scatter_dimension=0, tiled=True)
+    wave_size = lax.axis_size("wave")
+    summed = scatter_sum(partial.reshape(wave_size, case_count // wave_size, own_buildings), "wave", 1)
     return summed.T / counts_own.astype(jnp.float32)[:, None]
 
 

time: 153 us -> 51.5 us (0.34)
  waiting for transfers between devices: 113 us -> 0 us
  Pallas kernels: 0 us -> 26.3 us
  between operations: 14.2 us -> 0.17 us
    unnamed x3 -> x0, waiting for transfers between devices: 101 us -> none
    pallas_call x0 -> x2, Pallas kernels: none -> 26.3 us  [scatter_sum(): pl.pallas_call(kernel, out_shape=jax.ShapeDtypeStruct(block, x.dtype), in...]
    reduce_scatter x1 -> x0, waiting for transfers between devices: 12.1 us -> none  [body(): v_own = lax.psum_scatter(v_part, 'dof', scatter_dimension=0, tiled=True)]
  transfers between devices with their start and end apart: 2 -> 0, of which waited for: 2 -> 0; matrix products, arithmetic and copies ran while one was open for 8% -> 0% of each run, Pallas kernels for 0% -> 0%
where the time goes in v2:
time: 51.5 us; the launch traced here: 51.2 us
  Pallas kernels  26.3 us (51%)
  other arithmetic  13.1 us (25%)
  matrix products  7.78 us (15%)
  local copies, waits for them, and re-layouts  3.89 us (8%)
    pallas_call x2, Pallas kernels, scatter_sum(): pl.pallas_call(kernel, out_shape=jax.ShapeDtypeStruct(block, x.dtype), in...  26.3 us
    dot_general x1, matrix products, body(): jnp.einsum('mkj,gmji->gmki', lhs, green, preferred_element_type=jnp.float32)  7.12 us
    reduce_sum x1, other arithmetic, body(): phase_re = jnp.sum(axle_load[None] * jnp.cos(angle), axis=2) * norm_axle  4.9 us
    reduce_sum x1, other arithmetic, body(): w_im = jnp.sum(used[:, :, None] * t_im, axis=1)  4.49 us
    div x1, other arithmetic, body(): return summed.T / counts_own.astype(jnp.float32)[:, None]  1.29 us
    add x1, other arithmetic, body(): a_part = w_re * v_re + w_im * v_im  1.1 us

profile of v2, /device:TPU:1, one launch (start us, length us, event | category | flops | bytes accessed | tf_op | source)
XLA Modules:
  0.0 51.2 jit_solution(5977209319046693831)
XLA Ops:
  0.0 0.0 copy-start
  0.0 0.0 copy-start.2
  0.0 0.0 copy-start.1
  0.0 1.0 %fusion.37 = (f32[1,64,512]{2,1,0:T(8,128)S(1)}, f32[1,64,512]{2,1,0:T(8,128)S(1)}) fusion(f32[2,64,512]{2,1,0:T(8,128)} %param.8), kind=kLoop, calls=%fused_computation.71 | loop fusion | bytes 524288 | tf_op jit(solution)/shard_map/slice | solution.py:80
  1.0 0.3 subtract_convert_fusion
  1.3 0.3 fusion.21
  1.6 7.1 %fusion.2 = f32[2,64,4,128]{3,2,0,1:T(4,128)S(1)} fusion(bf16[2,64,512,128]{3,2,1,0:T(8,128)(2,1)} %param.7, bf16[64,1,512]{2,1,0:T(2,128)(2,1)S(1)} %get-tuple-element.20, bf16[64,1,512]{2,1,0:T(2,128)(2,1)S(1)} %get-tuple-element.23, bf16[64,1,512]{2,1,0:T(2,128)(2,1)S(1)} %get-tuple-element.21, bf16[64,1,512]{2,1,0:T(2,128)(2,1)S(1)} %get-tuple-element.22), kind=kOutput, calls=%fused_computation.13 | convolution fusion | flops 68157440 | bytes 17301504 | tf_op jit(solution)/shard_map/mkj,gmji->gmki/dot_general | solution.py:83
  8.7 0.2 fusion.36
  8.9 0.0 copy-done
  8.9 0.3 convolution_bitcast_fusion
  9.2 0.1 slice_add_fusion
  9.3 1.0 %copy.26 = f32[1024,128]{1,0:T(8,128)} copy(f32[1024,128]{0,1:T(8,128)S(1)} %slice_add_fusion) | data formatting | bytes 1048576 | tf_op jit(solution)/shard_map/add | solution.py:93
  10.3 12.2 %shard_map.73 = f32[256,128]{1,0:T(8,128)} custom-call(f32[4,256,128]{2,1,0:T(8,128)} %bitcast.36), custom_call_target="tpu_custom_call" | custom-call | tf_op jit(solution)/shard_map/pallas_call | solution.py:51
  22.5 0.8 %fusion.35 = (f32[256]{0:T(256)S(1)}, s32[256]{0:T(256)S(1)}) fusion(s32[1024]{0:T(1024)} %param.12, s32[]{:T(128)S(6)} %select_n.18), kind=kLoop, calls=%fused_computation.69 | loop fusion | flops 256 | bytes 3076 | tf_op jit(solution)/shard_map/convert_element_type | solution.py:119
  23.3 0.7 %constant_dynamic-slice_fusion = s32[256,16]{0,1:T(8,128)S(1)} fusion(s32[1024,16]{0,1:T(8,128)} %param.11, s32[]{:T(128)S(6)} %select_n.18), kind=kLoop, calls=%fused_computation.65 | loop fusion | bytes 32772 | tf_op jit(solution)/shard_map/dynamic_slice | solution.py:99
  24.0 4.5 %multiply_reduce_fusion = (f32[256,64]{0,1:T(8,128)S(1)}, f32[256,64]{0,1:T(8,128)S(1)}) fusion(s32[64]{0:T(128)S(1)} %iota_add_fusion, s32[256,16]{0,1:T(8,128)S(1)} %constant_dynamic-slice_fusion, f32[256,16]{0,1:T(8,128)S(1)} %fusion.31), kind=kLoop, calls=%fused_computation.20 | loop fusion | flops 6520832 | bytes 164096 | tf_op jit(solution)/shard_map/reduce_sum | solution.py:108
  28.5 0.1 copy.27
  28.6 0.1 copy.28
  28.7 1.1 %multiply_add_fusion = (f32[256,64]{1,0:T(8,128)S(1)}, f32[256,64]{1,0:T(8,128)S(1)}) fusion(f32[256,64]{1,0:T(8,128)S(1)} %copy.28, f32[256,64]{1,0:T(8,128)S(1)} %copy.27, f32[256,128]{1,0:T(8,128)} %shard_map.73), kind=kLoop, calls=%fused_computation.41 | loop fusion | flops 98304 | bytes 393216 | tf_op jit(solution)/shard_map/add | solution.py:110
  29.8 0.0 copy-done.2
  29.8 0.0 copy-done.1
  29.9 4.9 %multiply_reduce_fusion.3 = (f32[64,128]{1,0:T(8,128)S(1)}, f32[64,128]{1,0:T(8,128)S(1)}) fusion(s32[128,32]{0,1:T(8,128)S(1)} %copy-done.1, s32[64]{0:T(128)S(1)} %iota_add_fusion, f32[128,32]{0,1:T(8,128)S(1)} %copy-done.2), kind=kLoop, calls=%fused_computation.25 | loop fusion | flops 4702208 | bytes 98560 | tf_op jit(solution)/shard_map/reduce_sum | solution.py:77
  34.8 0.4 fusion.17
  35.2 0.7 %reshape.105.x_ref = f32[32,4,256]{2,1,0:T(4,128)} reshape(f32[128,256]{1,0:T(8,128)S(1)} %fusion.17) | data formatting | bytes 262144 | tf_op jit(solution)/shard_map/reshape | solution.py:118
  35.8 14.0 %shard_map.74 = f32[4,256]{1,0:T(4,128)} custom-call(f32[32,4,256]{2,1,0:T(4,128)} %reshape.105.x_ref), custom_call_target="tpu_custom_call" | custom-call | tf_op jit(solution)/shard_map/pallas_call | solution.py:51
  49.9 1.3 %divide_bitcast_fusion = f32[256,4]{0,1:T(4,128)} fusion(f32[4,256]{1,0:T(4,128)} %shard_map.74, f32[256]{0:T(256)S(1)} %get-tuple-element.9), kind=kLoop, calls=%fused_computation.63 | loop fusion | flops 1024 | bytes 9216 | tf_op jit(solution)/shard_map/div | solution.py:119
  (6 shorter events, 0.0 us)
Async XLA Ops:
  0.0 8.9 %copy-start = (bf16[1024,128]{1,0:T(8,128)(2,1)S(1)}, bf16[1024,128]{1,0:T(8,128)(2,1)}, u32[]{:S(2)}) copy-start(bf16[1024,128]{1,0:T(8,128)(2,1)} %param.13) | copy-start | bytes 786436
  0.0 29.8 %copy-start.2 = (f32[128,32]{0,1:T(8,128)S(1)}, f32[128,32]{0,1:T(8,128)}, u32[]{:S(2)}) copy-start(f32[128,32]{0,1:T(8,128)} %param.10) | copy-start | bytes 49156
  0.0 29.8 %copy-start.1 = (s32[128,32]{0,1:T(8,128)S(1)}, s32[128,32]{0,1:T(8,128)}, u32[]{:S(2)}) copy-start(s32[128,32]{0,1:T(8,128)} %param.9) | copy-start | bytes 49156

commit v3 on v2

--- a/solution.py
+++ b/solution.py
@@ -62,20 +62,92 @@
     )(x)
 
 
+def dof_exchange(vt, rows_t, used_t, pos_t, load_t, wave_count):
+    n = lax.axis_size("dof")
+    modes = vt.shape[0]
+    own = vt.shape[1] // n
+    slots, cases = rows_t.shape[0], pos_t.shape[1]
+    axles = pos_t.shape[0]
+    mesh_id = pl.DeviceIdType.MESH
+    step = 2.0 * math.pi / K
+    scale = 1.0 / math.sqrt(K)
+    norm_axle = 1.0 / math.sqrt(axles)
+
+    def kernel(vt_ref, rows_ref, used_ref, pos_ref, load_ref, ab_ref, phase_ref, recv, send_sems, recv_sems):
+        me = lax.axis_index("dof")
+        barrier = pltpu.get_barrier_semaphore()
+        for k in range(1, n):
+            pl.semaphore_signal(barrier, inc=1, device_id={"dof": lax.rem(me + k, n)}, device_id_type=mesh_id)
+        pl.semaphore_wait(barrier, n - 1)
+        copies = []
+        for k in range(1, n):
+            peer = lax.rem(me + k, n)
+            copy = pltpu.make_async_remote_copy(
+                src_ref=vt_ref.at[:, pl.ds(pl.multiple_of(peer * own, own), own)],
+                dst_ref=recv.at[k - 1],
+                send_sem=send_sems.at[k - 1],
+                recv_sem=recv_sems.at[k - 1],
+                device_id={"dof": peer},
+                device_id_type=mesh_id,
+            )
+            copy.start()
+            copies.append(copy)
+
+        m_col = lax.axis_index("wave") * wave_count + lax.broadcasted_iota(jnp.int32, (wave_count, 1), 0)
+        w_re = jnp.zeros((wave_count, own), jnp.float32)
+        w_im = jnp.zeros((wave_count, own), jnp.float32)
+        for s in range(slots):
+            angle = ((m_col * rows_ref[s : s + 1, :]) & (K - 1)).astype(jnp.float32) * step
+            t_re = (jnp.cos(angle) * scale).astype(jnp.bfloat16).astype(jnp.float32)
+            t_im = (-jnp.sin(angle) * scale).astype(jnp.bfloat16).astype(jnp.float32)
+            used = used_ref[s : s + 1, :]
+            w_re = w_re + used * t_re
+            w_im = w_im + used * t_im
+        p_re = jnp.zeros((wave_count, cases), jnp.float32)
+        p_im = jnp.zeros((wave_count, cases), jnp.float32)
+        for a in range(axles):
+            angle = ((m_col * pos_ref[a : a + 1, :]) & (K - 1)).astype(jnp.float32) * step
+            load = load_ref[a : a + 1, :]
+            p_re = p_re + load * jnp.cos(angle)
+            p_im = p_im + load * jnp.sin(angle)
+        phase_ref[0:wave_count, :] = p_re * norm_axle
+        phase_ref[wave_count : 2 * wave_count, :] = -p_im * norm_axle
+
+        for copy in copies:
+            copy.wait()
+        total = vt_ref[:, pl.ds(pl.multiple_of(me * own, own), own)]
+        for k in range(n - 1):
+            total = total + recv[k]
+        v_re = total[0:wave_count]
+        v_im = total[wave_count : 2 * wave_count]
+        ab_ref[0:wave_count, :] = w_re * v_re + w_im * v_im
+        ab_ref[wave_count : 2 * wave_count, :] = w_im * v_re - w_re * v_im
+
+    return pl.pallas_call(
+        kernel,
+        out_shape=(
+            jax.ShapeDtypeStruct((modes, own), jnp.float32),
+            jax.ShapeDtypeStruct((2 * wave_count, cases), jnp.float32),
+        ),
+        in_specs=[pl.BlockSpec(memory_space=pltpu.VMEM)] * 5,
+        out_specs=(pl.BlockSpec(memory_space=pltpu.VMEM), pl.BlockSpec(memory_space=pltpu.VMEM)),
+        scratch_shapes=[
+            pltpu.VMEM((n - 1, modes, own), jnp.float32),
+            pltpu.SemaphoreType.DMA((n - 1,)),
+            pltpu.SemaphoreType.DMA((n - 1,)),
+        ],
+        compiler_params=pltpu.CompilerParams(collective_id=0, has_side_effects=True),
+    )(vt, rows_t, used_t, pos_t, load_t)
+
+
 def body(green, rough, axle_pos, axle_load, rows, counts, coupling):
     wave_count = green.shape[1]
     case_count = axle_pos.shape[0]
     building_count = rows.shape[0]
     slot_count = rows.shape[1]
     dof_size = lax.axis_size("dof")
+    wave_size = lax.axis_size("wave")
     own_buildings = building_count // dof_size
-    waves = lax.axis_index("wave") * wave_count + jnp.arange(wave_count, dtype=jnp.int32)
-
-    product = waves[:, None, None] * axle_pos[None, :, :] % K
-    angle = product.astype(jnp.float32) * (2.0 * math.pi / K)
-    norm_axle = 1.0 / math.sqrt(axle_pos.shape[1])
-    phase_re = jnp.sum(axle_load[None] * jnp.cos(angle), axis=2) * norm_axle
-    phase_im = -jnp.sum(axle_load[None] * jnp.sin(angle), axis=2) * norm_axle
 
     re_hi, re_lo = split_bf16(rough[0])
     im_hi, im_lo = split_bf16(rough[1])
@@ -89,32 +161,19 @@
 
     h_hi, h_lo = split_bf16(h_cat)
     rhs = jnp.concatenate([h_hi, h_lo], axis=0)
-    both = jnp.einsum("bi,ni->bn", coupling, rhs, preferred_element_type=jnp.float32)
-    v_part = both[:, : 2 * wave_count] + both[:, 2 * wave_count :]
-    v_own = scatter_sum(v_part.reshape(dof_size, own_buildings, 2 * wave_count), "dof", 0)
-    v_re = v_own[:, :wave_count]
-    v_im = v_own[:, wave_count:]
+    both = jnp.einsum("ni,bi->nb", rhs, coupling, preferred_element_type=jnp.float32)
+    vt_part = both[: 2 * wave_count] + both[2 * wave_count :]
 
     first = lax.axis_index("dof") * own_buildings
     rows_own = lax.dynamic_slice_in_dim(rows, first, own_buildings, 0)
     counts_own = lax.dynamic_slice_in_dim(counts, first, own_buildings, 0)
     used = (jnp.arange(slot_count, dtype=jnp.int32)[None, :] < counts_own[:, None]).astype(jnp.float32)
-    station_prod = rows_own[:, :, None] * waves[None, None, :] % K
-    station_angle = station_prod.astype(jnp.float32) * (2.0 * math.pi / K)
-    scale = 1.0 / math.sqrt(K)
-    t_re = (jnp.cos(station_angle) * scale).astype(jnp.bfloat16).astype(jnp.float32)
-    t_im = (-jnp.sin(station_angle) * scale).astype(jnp.bfloat16).astype(jnp.float32)
-    w_re = jnp.sum(used[:, :, None] * t_re, axis=1)
-    w_im = jnp.sum(used[:, :, None] * t_im, axis=1)
+    ab_t, phase_cat = dof_exchange(vt_part, rows_own.T, used.T, axle_pos.T, axle_load.T, wave_count)
 
-    a_part = w_re * v_re + w_im * v_im
-    b_part = w_im * v_re - w_re * v_im
-    ab = jnp.concatenate([a_part, b_part], axis=1)
-    phase_cat = jnp.concatenate([phase_re, phase_im], axis=0)
-    partial = jnp.dot(
-        phase_cat.T, ab.T, precision=lax.Precision.HIGHEST, preferred_element_type=jnp.float32
+    partial = lax.dot_general(
+        phase_cat, ab_t, (((0,), (0,)), ((), ())),
+        precision=lax.Precision.HIGHEST, preferred_element_type=jnp.float32,
     )
-    wave_size = lax.axis_size("wave")
     summed = scatter_sum(partial.reshape(wave_size, case_count // wave_size, own_buildings), "wave", 1)
     return summed.T / counts_own.astype(jnp.float32)[:, None]
 

time: 51.5 us -> 43.8 us (0.85)
  other arithmetic: 13.1 us -> 3.96 us
  Pallas kernels: 26.3 us -> 27.5 us
  matrix products: 7.78 us -> 8.67 us
  local copies, waits for them, and re-layouts: 3.89 us -> 3.3 us
    pallas_call x0 -> x1, Pallas kernels: none -> 14.1 us  [dof_exchange(): pl.pallas_call(kernel, out_shape=(jax.ShapeDtypeStruct((modes, own), jnp....]
    pallas_call x2 -> x1, Pallas kernels: 26.3 us -> 13.4 us  [scatter_sum(): pl.pallas_call(kernel, out_shape=jax.ShapeDtypeStruct(block, x.dtype), in...]
    reduce_sum x2 -> x0, other arithmetic: 9.39 us -> none  [the longest x1 4.9 us: body(): phase_re = jnp.sum(axle_load[None] * jnp.cos(angle), axis=2) * norm_axle]
    transpose x0 -> x1, local copies, waits for them, and re-layouts: none -> 1.31 us  [body(): ab_t, phase_cat = dof_exchange(vt_part, rows_own.T, used.T, axle_pos.T, a...]
    add x1 -> x0, local copies, waits for them, and re-layouts: 0.99 us -> none  [body(): v_part = both[:, :2 * wave_count] + both[:, 2 * wave_count:]]
    dot_general x2, matrix products: 0.66 us -> 1.55 us  [the longest x1 1.25 us: body(): lax.dot_general(phase_cat, ab_t, (((0,), (0,)), ((), ())), precision=lax....]
    dynamic_slice x1 -> x0, local copies, waits for them, and re-layouts: 0.72 us -> none  [body(): rows_own = lax.dynamic_slice_in_dim(rows, first, own_buildings, 0)]
    convert_element_type x1, other arithmetic: 0.01 us -> 0.61 us  [body(): (jnp.arange(slot_count, dtype=jnp.int32)[None, :] < counts_own[:, None])....]
where the time goes in v3:
time: 43.8 us; the launch traced here: 43.5 us
  Pallas kernels  27.5 us (63%)
  matrix products  8.67 us (20%)
  other arithmetic  3.96 us (9%)
  local copies, waits for them, and re-layouts  3.3 us (8%)
    pallas_call x1, Pallas kernels, dof_exchange(): pl.pallas_call(kernel, out_shape=(jax.ShapeDtypeStruct((modes, own), jnp....  14.1 us
    pallas_call x1, Pallas kernels, scatter_sum(): pl.pallas_call(kernel, out_shape=jax.ShapeDtypeStruct(block, x.dtype), in...  13.4 us
    dot_general x1, matrix products, body(): jnp.einsum('mkj,gmji->gmki', lhs, green, preferred_element_type=jnp.float32)  7.12 us
    transpose x1, local copies, waits for them, and re-layouts, body(): ab_t, phase_cat = dof_exchange(vt_part, rows_own.T, used.T, axle_pos.T, a...  1.31 us
    div x1, other arithmetic, body(): return summed.T / counts_own.astype(jnp.float32)[:, None]  1.28 us
    dot_general x1, matrix products, body(): lax.dot_general(phase_cat, ab_t, (((0,), (0,)), ((), ())), precision=lax....  1.25 us
    slice x1, local copies, waits for them, and re-layouts, body(): re_hi, re_lo = split_bf16(rough[0])  1.03 us

profile of v3, /device:TPU:1, one launch (start us, length us, event | category | flops | bytes accessed | tf_op | source)
XLA Modules:
  0.0 43.5 jit_solution(15512185397756211595)
XLA Ops:
  0.0 0.0 copy-start
  0.0 1.0 %fusion.24 = (f32[1,64,512]{2,1,0:T(8,128)S(1)}, f32[1,64,512]{2,1,0:T(8,128)S(1)}) fusion(f32[2,64,512]{2,1,0:T(8,128)} %param.8), kind=kLoop, calls=%fused_computation.36 | loop fusion | bytes 524288 | tf_op jit(solution)/shard_map/slice | solution.py:152
  1.0 0.3 fusion.11
  1.3 0.3 subtract_convert_fusion
  1.6 7.1 %fusion.2 = f32[2,64,4,128]{3,2,0,1:T(4,128)S(1)} fusion(bf16[2,64,512,128]{3,2,1,0:T(8,128)(2,1)} %param.7, bf16[64,1,512]{2,1,0:T(2,128)(2,1)S(1)} %get-tuple-element.18, bf16[64,1,512]{2,1,0:T(2,128)(2,1)S(1)} %get-tuple-element.21, bf16[64,1,512]{2,1,0:T(2,128)(2,1)S(1)} %get-tuple-element.19, bf16[64,1,512]{2,1,0:T(2,128)(2,1)S(1)} %get-tuple-element.20), kind=kOutput, calls=%fused_computation.2 | convolution fusion | flops 68157440 | bytes 17301504 | tf_op jit(solution)/shard_map/mkj,gmji->gmki/dot_general | solution.py:155
  8.7 0.2 fusion.23
  8.9 0.0 copy-done
  8.9 0.3 fusion.13
  9.2 0.9 %slice_add_fusion.vt_ref = f32[128,1024]{1,0:T(8,128)} fusion(f32[256,1024]{1,0:T(8,128)S(1)} %fusion.13), kind=kLoop, calls=%fused_computation.3 | loop fusion | flops 131072 | bytes 1572864 | tf_op jit(solution)/shard_map/add | solution.py:165
  10.1 0.8 %fusion.22 = (f32[256]{0:T(256)S(1)}, s32[256]{0:T(256)S(1)}) fusion(s32[1024]{0:T(1024)} %param.12, s32[]{:T(128)S(6)} %select_n.4), kind=kLoop, calls=%fused_computation.34 | loop fusion | flops 256 | bytes 3076 | tf_op jit(solution)/shard_map/convert_element_type | solution.py:178
  10.9 0.6 %fusion.19.used_ref = f32[16,256]{1,0:T(8,128)} fusion(s32[256]{0:T(256)S(1)} %get-tuple-element.10), kind=kLoop, calls=%fused_computation.30 | loop fusion | flops 8192 | bytes 17408 | tf_op jit(solution)/shard_map/convert_element_type | solution.py:170
  11.5 1.3 %dynamic-slice_bitcast_fusion.rows_ref = s32[16,256]{1,0:T(8,128)} fusion(s32[1024,16]{0,1:T(8,128)} %param.11, s32[]{:T(128)S(6)} %select_n.4), kind=kLoop, calls=%fused_computation.29 | loop fusion | bytes 32772 | tf_op jit(solution)/shard_map/transpose | solution.py:171
  12.8 14.1 %shard_map.73 = (f32[128,256]{1,0:T(8,128)}, f32[128,128]{1,0:T(8,128)}) custom-call(f32[128,1024]{1,0:T(8,128)} %slice_add_fusion.vt_ref, s32[16,256]{1,0:T(8,128)} %dynamic-slice_bitcast_fusion.rows_ref, f32[16,256]{1,0:T(8,128)} %fusion.19.used_ref, s32[32,128]{1,0:T(8,128)} %bitcast.45, f32[32,128]{1,0:T(8,128)} %bitcast.46), custom_call_target="tpu_custom_call" | custom-call | tf_op jit(solution)/shard_map/pallas_call | solution.py:126
  26.9 1.2 %fusion.25 = f32[128,256]{1,0:T(8,128)S(1)} fusion(f32[128,128]{1,0:T(8,128)} %get-tuple-element.7, f32[128,256]{1,0:T(8,128)} %get-tuple-element.8), kind=kOutput, calls=%fused_computation.37 | convolution fusion | flops 50331648 | bytes 327680 | tf_op jit(solution)/shard_map/dot_general | solution.py:173
  28.1 0.7 %reshape.69.x_ref = f32[32,4,256]{2,1,0:T(4,128)} reshape(f32[128,256]{1,0:T(8,128)S(1)} %fusion.25) | data formatting | bytes 262144 | tf_op jit(solution)/shard_map/reshape | solution.py:177
  28.8 13.4 %shard_map.74 = f32[4,256]{1,0:T(4,128)} custom-call(f32[32,4,256]{2,1,0:T(4,128)} %reshape.69.x_ref), custom_call_target="tpu_custom_call" | custom-call | tf_op jit(solution)/shard_map/pallas_call | solution.py:51
  42.3 1.3 %divide_bitcast_fusion = f32[256,4]{0,1:T(4,128)} fusion(f32[4,256]{1,0:T(4,128)} %shard_map.74, f32[256]{0:T(256)S(1)} %get-tuple-element.9), kind=kLoop, calls=%fused_computation.31 | loop fusion | flops 1024 | bytes 9216 | tf_op jit(solution)/shard_map/div | solution.py:178
  (3 shorter events, 0.0 us)
Async XLA Ops:
  0.0 8.9 %copy-start = (bf16[1024,128]{1,0:T(8,128)(2,1)S(1)}, bf16[1024,128]{1,0:T(8,128)(2,1)}, u32[]{:S(2)}) copy-start(bf16[1024,128]{1,0:T(8,128)(2,1)} %param.13) | copy-start | bytes 786436

commit v4 on v1

v4 whole, which is shorter than its diff:
```python
import math

import jax
import jax.numpy as jnp
from jax import lax
from jax.experimental import pallas as pl
from jax.experimental.pallas import tpu as pltpu
from jax.sharding import PartitionSpec as P

K = 2048


def split_bf16(x):
    hi = x.astype(jnp.bfloat16)
    lo = (x - hi.astype(jnp.float32)).astype(jnp.bfloat16)
    return hi, lo


def exchange(vt, rows_t, used_t, pos_t, load_t, wave_count):
    n_dof = lax.axis_size("dof")
    n_wave = lax.axis_size("wave")
    modes = vt.shape[0]
    own = vt.shape[1] // n_dof
    slots, cases = rows_t.shape[0], pos_t.shape[1]
    axles = pos_t.shape[0]
    per_wave = cases // n_wave
    pad = 8
    mesh_id = pl.DeviceIdType.MESH
    step = 2.0 * math.pi / K
    scale = 1.0 / math.sqrt(K)
    norm_axle = 1.0 / math.sqrt(axles)

    def kernel(vt_ref, rows_ref, used_ref, pos_ref, load_ref, out_ref,
               recv_v, send_r, recv_r, v_send, v_recv, r_send, r_recv):
        me_d = lax.axis_index("dof")
        me_w = lax.axis_index("wave")
        barrier = pltpu.get_barrier_semaphore()
        for k in range(1, n_dof):
            pl.semaphore_signal(barrier, inc=1, device_id={"dof": lax.rem(me_d + k, n_dof)}, device_id_type=mesh_id)
        for k in range(1, n_wave):
            pl.semaphore_signal(barrier, inc=1, device_id={"wave": lax.rem(me_w + k, n_wave)}, device_id_type=mesh_id)

        m_col = me_w * wave_count + lax.broadcasted_iota(jnp.int32, (wave_count, 1), 0)
        w_re = jnp.zeros((wave_count, own), jnp.float32)
        w_im = jnp.zeros((wave_count, own), jnp.float32)
        for s in range(slots):
            angle = ((m_col * rows_ref[s : s + 1, :]) & (K - 1)).astype(jnp.float32) * step
            t_re = (jnp.cos(angle) * scale).astype(jnp.bfloat16).astype(jnp.float32)
            t_im = (-jnp.sin(angle) * scale).astype(jnp.bfloat16).astype(jnp.float32)
            used = used_ref[s : s + 1, :]
            w_re = w_re + used * t_re
            w_im = w_im + used * t_im

        pl.semaphore_wait(barrier, n_dof - 1 + n_wave - 1)
        v_copies = []
        for k in range(1, n_dof):
            peer = lax.rem(me_d + k, n_dof)
            copy = pltpu.make_async_remote_copy(
                src_ref=vt_ref.at[:, pl.ds(pl.multiple_of(peer * own, own), own)],
                dst_ref=recv_v.at[k - 1],
                send_sem=v_send.at[k - 1],
                recv_sem=v_recv.at[k - 1],
                device_id={"dof": peer},
                device_id_type=mesh_id,
            )
            copy.start()
            v_copies.append(copy)

        p_re = jnp.zeros((wave_count, cases), jnp.float32)
        p_im = jnp.zeros((wave_count, cases), jnp.float32)
        for a in range(axles):
            angle = ((m_col * pos_ref[a : a + 1, :]) & (K - 1)).astype(jnp.float32) * step
            load = load_ref[a : a + 1, :]
            p_re = p_re + load * jnp.cos(angle)
            p_im = p_im + load * jnp.sin(angle)
        phase = jnp.concatenate([p_re * norm_axle, -p_im * norm_axle], axis=0)

        row = lax.broadcasted_iota(jnp.int32, (n_wave * pad, cases), 0)
        col = lax.broadcasted_iota(jnp.int32, (n_wave * pad, cases), 1)
        spread = jnp.where(
            (col == (row // pad) * per_wave + row % pad) & (row % pad < per_wave), 1.0, 0.0
        ).astype(jnp.bfloat16)
        ph_hi, ph_lo = split_bf16(phase)
        dims = (((1,), (1,)), ((), ()))
        pt_hi = lax.dot_general(spread, ph_hi, dims, preferred_element_type=jnp.float32).astype(jnp.bfloat16)
        pt_lo = lax.dot_general(spread, ph_lo, dims, preferred_element_type=jnp.float32).astype(jnp.bfloat16)

        for copy in v_copies:
            copy.wait()
        total = vt_ref[:, pl.ds(pl.multiple_of(me_d * own, own), own)]
        for k in range(n_dof - 1):
            total = total + recv_v[k]
        v_re = total[0:wave_count]
        v_im = total[wave_count : 2 * wave_count]
        ab = jnp.concatenate([w_re * v_re + w_im * v_im, w_im * v_re - w_re * v_im], axis=0)
        ab_hi, ab_lo = split_bf16(ab)
        r_pad = (
            jnp.dot(pt_hi, ab_hi, preferred_element_type=jnp.float32)
            + jnp.dot(pt_hi, ab_lo, preferred_element_type=jnp.float32)
            + jnp.dot(pt_lo, ab_hi, preferred_element_type=jnp.float32)
        )
        for p in range(n_wave):
            send_r[p] = r_pad[p * pad : (p + 1) * pad]
        result = send_r[me_w]

        r_copies = []
        for k in range(1, n_wave):
            peer = lax.rem(me_w + k, n_wave)
            copy = pltpu.make_async_remote_copy(
                src_ref=send_r.at[peer],
                dst_ref=recv_r.at[k - 1],
                send_sem=r_send.at[k - 1],
                recv_sem=r_recv.at[k - 1],
                device_id={"wave": peer},
                device_id_type=mesh_id,
            )
            copy.start()
            r_copies.append(copy)
        for copy in r_copies:
            copy.wait()
        for k in range(n_wave - 1):
            result = result + recv_r[k]
        out_ref[...] = result

    return pl.pallas_call(
        kernel,
        out_shape=jax.ShapeDtypeStruct((pad, own), jnp.float32),
        in_specs=[pl.BlockSpec(memory_space=pltpu.VMEM)] * 5,
        out_specs=pl.BlockSpec(memory_space=pltpu.VMEM),
        scratch_shapes=[
            pltpu.VMEM((n_dof - 1, modes, own), jnp.float32),
            pltpu.VMEM((n_wave, pad, own), jnp.float32),
            pltpu.VMEM((n_wave - 1, pad, own), jnp.float32),
            pltpu.SemaphoreType.DMA((n_dof - 1,)),
            pltpu.SemaphoreType.DMA((n_dof - 1,)),
            pltpu.SemaphoreType.DMA((n_wave - 1,)),
            pltpu.SemaphoreType.DMA((n_wave - 1,)),
        ],
        compiler_params=pltpu.CompilerParams(collective_id=0, has_side_effects=True),
    )(vt, rows_t, used_t, pos_t, load_t)


def body(green, rough, axle_pos, axle_load, rows, counts, coupling):
    wave_count = green.shape[1]
    case_count = axle_pos.shape[0]
    building_count = rows.shape[0]
    slot_count = rows.shape[1]
    dof_size = lax.axis_size("dof")
    wave_size = lax.axis_size("wave")
    own_buildings = building_count // dof_size

    re_hi, re_lo = split_bf16(rough[0])
    im_hi, im_lo = split_bf16(rough[1])
    lhs = jnp.stack([re_hi, re_lo, im_hi, im_lo], axis=1)
    prod = jnp.einsum("mkj,gmji->gmki", lhs, green, preferred_element_type=jnp.float32)
    gre_rre = prod[0, :, 0] + prod[0, :, 1]
    gre_rim = prod[0, :, 2] + prod[0, :, 3]
    gim_rre = prod[1, :, 0] + prod[1, :, 1]
    gim_rim = prod[1, :, 2] + prod[1, :, 3]
    h_cat = jnp.concatenate([gre_rre - gim_rim, gre_rim + gim_rre], axis=0)

    h_hi, h_lo = split_bf16(h_cat)
    rhs = jnp.concatenate([h_hi, h_lo], axis=0)
    both = jnp.einsum("ni,bi->nb", rhs, coupling, preferred_element_type=jnp.float32)
    vt_part = both[: 2 * wave_count] + both[2 * wave_count :]

    first = lax.axis_index("dof") * own_buildings
    rows_own = lax.dynamic_slice_in_dim(rows, first, own_buildings, 0)
    counts_own = lax.dynamic_slice_in_dim(counts, first, own_buildings, 0)
    used = (jnp.arange(slot_count, dtype=jnp.int32)[None, :] < counts_own[:, None]).astype(jnp.float32)
    summed = exchange(vt_part, rows_own.T, used.T, axle_pos.T, axle_load.T, wave_count)
    per_wave = case_count // wave_size
    return summed[:per_wave].T / counts_own.astype(jnp.float32)[:, None]


def solution(mesh):
    in_specs = (
        P(None, "wave", None, "dof"),
        P(None, "wave", None),
        P(),
        P(),
        P(),
        P(),
        P(None, "dof"),
    )
    out_specs = P("dof", "wave")
    return jax.shard_map(body, mesh=mesh, in_specs=in_specs, out_specs=out_specs, check_vma=False)
```

time: 153 us -> 41 us (0.27)
  waiting for transfers between devices: 113 us -> 0 us
  Pallas kernels: 0 us -> 26.7 us
  between operations: 14.2 us -> 0.07 us
  other arithmetic: 13.7 us -> 3.96 us
    unnamed x3 -> x0, waiting for transfers between devices: 101 us -> none
    pallas_call x0 -> x1, Pallas kernels: none -> 26.7 us  [exchange(): pl.pallas_call(kernel, out_shape=jax.ShapeDtypeStruct((pad, own), jnp.flo...]
    reduce_scatter x1 -> x0, waiting for transfers between devices: 12.1 us -> none  [body(): v_own = lax.psum_scatter(v_part, 'dof', scatter_dimension=0, tiled=True)]
    reduce_sum x2 -> x0, other arithmetic: 9.4 us -> none  [the longest x1 4.91 us: body(): phase_re = jnp.sum(axle_load[None] * jnp.cos(angle), axis=2) * norm_axle]
  transfers between devices with their start and end apart: 2 -> 0, of which waited for: 2 -> 0; matrix products, arithmetic and copies ran while one was open for 8% -> 0% of each run, Pallas kernels for 0% -> 0%
where the time goes in v4:
time: 41 us; the launch traced here: 40.7 us
  Pallas kernels  26.7 us (65%)
  matrix products  7.42 us (18%)
  other arithmetic  3.96 us (10%)
  local copies, waits for them, and re-layouts  2.62 us (6%)
    pallas_call x1, Pallas kernels, exchange(): pl.pallas_call(kernel, out_shape=jax.ShapeDtypeStruct((pad, own), jnp.flo...  26.7 us
    dot_general x1, matrix products, body(): jnp.einsum('mkj,gmji->gmki', lhs, green, preferred_element_type=jnp.float32)  7.12 us
    transpose x1, local copies, waits for them, and re-layouts, body(): summed = exchange(vt_part, rows_own.T, used.T, axle_pos.T, axle_load.T, w...  1.32 us
    div x1, other arithmetic, body(): return summed[:per_wave].T / counts_own.astype(jnp.float32)[:, None]  1.3 us
    slice x1, local copies, waits for them, and re-layouts, body(): re_hi, re_lo = split_bf16(rough[0])  1.03 us
    add x1, other arithmetic, body(): vt_part = both[:2 * wave_count] + both[2 * wave_count:]  0.85 us

profile of v4, /device:TPU:1, one launch (start us, length us, event | category | flops | bytes accessed | tf_op | source)
XLA Modules:
  0.0 40.7 jit_solution(16184066071566919416)
XLA Ops:
  0.0 0.0 copy-start
  0.0 1.0 %fusion.24 = (f32[1,64,512]{2,1,0:T(8,128)S(1)}, f32[1,64,512]{2,1,0:T(8,128)S(1)}) fusion(f32[2,64,512]{2,1,0:T(8,128)} %param.8), kind=kLoop, calls=%fused_computation.36 | loop fusion | bytes 524288 | tf_op jit(solution)/shard_map/slice | solution.py:152
  1.0 0.3 fusion.11
  1.3 0.3 subtract_convert_fusion
  1.6 7.1 %fusion.2 = f32[2,64,4,128]{3,2,0,1:T(4,128)S(1)} fusion(bf16[2,64,512,128]{3,2,1,0:T(8,128)(2,1)} %param.7, bf16[64,1,512]{2,1,0:T(2,128)(2,1)S(1)} %get-tuple-element.14, bf16[64,1,512]{2,1,0:T(2,128)(2,1)S(1)} %get-tuple-element.17, bf16[64,1,512]{2,1,0:T(2,128)(2,1)S(1)} %get-tuple-element.15, bf16[64,1,512]{2,1,0:T(2,128)(2,1)S(1)} %get-tuple-element.16), kind=kOutput, calls=%fused_computation.2 | convolution fusion | flops 68157440 | bytes 17301504 | tf_op jit(solution)/shard_map/mkj,gmji->gmki/dot_general | solution.py:155
  8.7 0.2 fusion.23
  8.9 0.0 copy-done
  8.9 0.3 fusion.13
  9.2 0.9 %slice_add_fusion.vt_ref = f32[128,1024]{1,0:T(8,128)} fusion(f32[256,1024]{1,0:T(8,128)S(1)} %fusion.13), kind=kLoop, calls=%fused_computation.3 | loop fusion | flops 131072 | bytes 1572864 | tf_op jit(solution)/shard_map/add | solution.py:165
  10.1 0.8 %fusion.22 = (f32[256]{0:T(256)S(1)}, s32[256]{0:T(256)S(1)}) fusion(s32[1024]{0:T(1024)} %param.12, s32[]{:T(128)S(6)} %select_n.4), kind=kLoop, calls=%fused_computation.34 | loop fusion | flops 256 | bytes 3076 | tf_op jit(solution)/shard_map/convert_element_type | solution.py:173
  10.9 0.6 %fusion.19.used_ref = f32[16,256]{1,0:T(8,128)} fusion(s32[256]{0:T(256)S(1)} %get-tuple-element.6), kind=kLoop, calls=%fused_computation.30 | loop fusion | flops 8192 | bytes 17408 | tf_op jit(solution)/shard_map/convert_element_type | solution.py:170
  11.5 1.3 %dynamic-slice_bitcast_fusion.rows_ref = s32[16,256]{1,0:T(8,128)} fusion(s32[1024,16]{0,1:T(8,128)} %param.11, s32[]{:T(128)S(6)} %select_n.4), kind=kLoop, calls=%fused_computation.29 | loop fusion | bytes 32772 | tf_op jit(solution)/shard_map/transpose | solution.py:171
  12.8 26.7 %shard_map.73 = f32[8,256]{1,0:T(8,128)} custom-call(f32[128,1024]{1,0:T(8,128)} %slice_add_fusion.vt_ref, s32[16,256]{1,0:T(8,128)} %dynamic-slice_bitcast_fusion.rows_ref, f32[16,256]{1,0:T(8,128)} %fusion.19.used_ref, s32[32,128]{1,0:T(8,128)} %bitcast.43, f32[32,128]{1,0:T(8,128)} %bitcast.44), custom_call_target="tpu_custom_call" | custom-call | tf_op jit(solution)/shard_map/pallas_call | solution.py:125
  39.4 1.3 %divide_bitcast_fusion = f32[256,4]{0,1:T(4,128)} fusion(f32[8,256]{1,0:T(8,128)} %shard_map.73, f32[256]{0:T(256)S(1)} %get-tuple-element.5), kind=kLoop, calls=%fused_computation.31 | loop fusion | flops 1024 | bytes 9216 | tf_op jit(solution)/shard_map/div | solution.py:173
  (3 shorter events, 0.0 us)
Async XLA Ops:
  0.0 8.9 %copy-start = (bf16[1024,128]{1,0:T(8,128)(2,1)S(1)}, bf16[1024,128]{1,0:T(8,128)(2,1)}, u32[]{:S(2)}) copy-start(bf16[1024,128]{1,0:T(8,128)(2,1)} %param.13) | copy-start | bytes 786436

commit v5 on v4

--- a/solution.py
+++ b/solution.py
@@ -16,7 +16,7 @@
     return hi, lo
 
 
-def exchange(vt, rows_t, used_t, pos_t, load_t, wave_count):
+def exchange(vt, rows_t, pos_t, load_t, wave_count):
     n_dof = lax.axis_size("dof")
     n_wave = lax.axis_size("wave")
     modes = vt.shape[0]
@@ -30,7 +30,7 @@
     scale = 1.0 / math.sqrt(K)
     norm_axle = 1.0 / math.sqrt(axles)
 
-    def kernel(vt_ref, rows_ref, used_ref, pos_ref, load_ref, out_ref,
+    def kernel(vt_ref, rows_ref, pos_ref, load_ref, out_ref,
                recv_v, send_r, recv_r, v_send, v_recv, r_send, r_recv):
         me_d = lax.axis_index("dof")
         me_w = lax.axis_index("wave")
@@ -43,11 +43,14 @@
         m_col = me_w * wave_count + lax.broadcasted_iota(jnp.int32, (wave_count, 1), 0)
         w_re = jnp.zeros((wave_count, own), jnp.float32)
         w_im = jnp.zeros((wave_count, own), jnp.float32)
+        count = jnp.zeros((1, own), jnp.float32)
         for s in range(slots):
-            angle = ((m_col * rows_ref[s : s + 1, :]) & (K - 1)).astype(jnp.float32) * step
+            station = rows_ref[s : s + 1, :]
+            angle = ((m_col * station) & (K - 1)).astype(jnp.float32) * step
             t_re = (jnp.cos(angle) * scale).astype(jnp.bfloat16).astype(jnp.float32)
             t_im = (-jnp.sin(angle) * scale).astype(jnp.bfloat16).astype(jnp.float32)
-            used = used_ref[s : s + 1, :]
+            used = jnp.where(station >= 0, 1.0, 0.0)
+            count = count + used
             w_re = w_re + used * t_re
             w_im = w_im + used * t_im
 
@@ -107,8 +110,8 @@
         for k in range(1, n_wave):
             peer = lax.rem(me_w + k, n_wave)
             copy = pltpu.make_async_remote_copy(
-                src_ref=send_r.at[peer],
-                dst_ref=recv_r.at[k - 1],
+                src_ref=send_r.at[peer, 0:per_wave],
+                dst_ref=recv_r.at[k - 1, 0:per_wave],
                 send_sem=r_send.at[k - 1],
                 recv_sem=r_recv.at[k - 1],
                 device_id={"wave": peer},
@@ -118,14 +121,15 @@
             r_copies.append(copy)
         for copy in r_copies:
             copy.wait()
+        result = result[0:per_wave]
         for k in range(n_wave - 1):
-            result = result + recv_r[k]
-        out_ref[...] = result
+            result = result + recv_r[k, 0:per_wave]
+        out_ref[...] = result / count
 
     return pl.pallas_call(
         kernel,
-        out_shape=jax.ShapeDtypeStruct((pad, own), jnp.float32),
-        in_specs=[pl.BlockSpec(memory_space=pltpu.VMEM)] * 5,
+        out_shape=jax.ShapeDtypeStruct((per_wave, own), jnp.float32),
+        in_specs=[pl.BlockSpec(memory_space=pltpu.VMEM)] * 4,
         out_specs=pl.BlockSpec(memory_space=pltpu.VMEM),
         scratch_shapes=[
             pltpu.VMEM((n_dof - 1, modes, own), jnp.float32),
@@ -137,7 +141,7 @@
             pltpu.SemaphoreType.DMA((n_wave - 1,)),
         ],
         compiler_params=pltpu.CompilerParams(collective_id=0, has_side_effects=True),
-    )(vt, rows_t, used_t, pos_t, load_t)
+    )(vt, rows_t, pos_t, load_t)
 
 
 def body(green, rough, axle_pos, axle_load, rows, counts, coupling):
@@ -167,10 +171,10 @@
     first = lax.axis_index("dof") * own_buildings
     rows_own = lax.dynamic_slice_in_dim(rows, first, own_buildings, 0)
     counts_own = lax.dynamic_slice_in_dim(counts, first, own_buildings, 0)
-    used = (jnp.arange(slot_count, dtype=jnp.int32)[None, :] < counts_own[:, None]).astype(jnp.float32)
-    summed = exchange(vt_part, rows_own.T, used.T, axle_pos.T, axle_load.T, wave_count)
-    per_wave = case_count // wave_size
-    return summed[:per_wave].T / counts_own.astype(jnp.float32)[:, None]
+    rows_used = jnp.where(
+        jnp.arange(slot_count, dtype=jnp.int32)[:, None] < counts_own[None, :], rows_own.T, -1
+    )
+    return exchange(vt_part, rows_used, axle_pos.T, axle_load.T, wave_count).T
 
 
 def solution(mesh):

time: 41 us -> 40 us (0.976)
  other arithmetic: 3.96 us -> 2.64 us
  local copies, waits for them, and re-layouts: 2.62 us -> 3.33 us
    convert_element_type x2 -> x0, other arithmetic: 1.36 us -> none  [the longest x1 0.76 us: body(): return summed[:per_wave].T / counts_own.astype(jnp.float32)[:, None]]
    select_n x0 -> x1, other arithmetic: none -> 1.32 us  [body(): jnp.where(jnp.arange(slot_count, dtype=jnp.int32)[:, None] < counts_own[N...]
    transpose x1 -> x0, local copies, waits for them, and re-layouts: 1.32 us -> none  [body(): summed = exchange(vt_part, rows_own.T, used.T, axle_pos.T, axle_load.T, w...]
    div x1 -> x0, other arithmetic: 1.3 us -> none  [body(): return summed[:per_wave].T / counts_own.astype(jnp.float32)[:, None]]
    unnamed x2 -> x3, local copies, waits for them, and re-layouts: 0.01 us -> 1.27 us
    dynamic_slice x0 -> x1, local copies, waits for them, and re-layouts: none -> 0.76 us  [body(): counts_own = lax.dynamic_slice_in_dim(counts, first, own_buildings, 0)]
where the time goes in v5:
time: 40 us; the launch traced here: 39.7 us
  Pallas kernels  26.3 us (66%)
  matrix products  7.42 us (19%)
  local copies, waits for them, and re-layouts  3.33 us (8%)
  other arithmetic  2.64 us (7%)
    pallas_call x1, Pallas kernels, exchange(): pl.pallas_call(kernel, out_shape=jax.ShapeDtypeStruct((per_wave, own), jn...  26.3 us
    dot_general x1, matrix products, body(): jnp.einsum('mkj,gmji->gmki', lhs, green, preferred_element_type=jnp.float32)  7.12 us
    select_n x1, other arithmetic, body(): jnp.where(jnp.arange(slot_count, dtype=jnp.int32)[:, None] < counts_own[N...  1.32 us
    unnamed x3, local copies, waits for them, and re-layouts  1.27 us
    slice x1, local copies, waits for them, and re-layouts, body(): re_hi, re_lo = split_bf16(rough[0])  1.03 us
    add x1, other arithmetic, body(): vt_part = both[:2 * wave_count] + both[2 * wave_count:]  0.86 us

profile of v5, /device:TPU:1, one launch (start us, length us, event | category | flops | bytes accessed | tf_op | source)
XLA Modules:
  0.0 39.7 jit_solution(4263085311195658064)
XLA Ops:
  0.0 0.0 copy-start
  0.0 1.0 %fusion.22 = (f32[1,64,512]{2,1,0:T(8,128)S(1)}, f32[1,64,512]{2,1,0:T(8,128)S(1)}) fusion(f32[2,64,512]{2,1,0:T(8,128)} %param.8), kind=kLoop, calls=%fused_computation.33 | loop fusion | bytes 524288 | tf_op jit(solution)/shard_map/slice | solution.py:156
  1.0 0.3 fusion.11
  1.3 0.3 subtract_convert_fusion
  1.6 7.1 %fusion.2 = f32[2,64,4,128]{3,2,0,1:T(4,128)S(1)} fusion(bf16[2,64,512,128]{3,2,1,0:T(8,128)(2,1)} %param.7, bf16[64,1,512]{2,1,0:T(2,128)(2,1)S(1)} %get-tuple-element.12, bf16[64,1,512]{2,1,0:T(2,128)(2,1)S(1)} %get-tuple-element.15, bf16[64,1,512]{2,1,0:T(2,128)(2,1)S(1)} %get-tuple-element.13, bf16[64,1,512]{2,1,0:T(2,128)(2,1)S(1)} %get-tuple-element.14), kind=kOutput, calls=%fused_computation.2 | convolution fusion | flops 68157440 | bytes 17301504 | tf_op jit(solution)/shard_map/mkj,gmji->gmki/dot_general | solution.py:159
  8.7 0.2 fusion.21
  8.9 0.0 copy-done
  8.9 0.3 fusion.13
  9.2 0.9 %slice_add_fusion.vt_ref = f32[128,1024]{1,0:T(8,128)} fusion(f32[256,1024]{1,0:T(8,128)S(1)} %fusion.13), kind=kLoop, calls=%fused_computation.3 | loop fusion | flops 131072 | bytes 1572864 | tf_op jit(solution)/shard_map/add | solution.py:169
  10.1 0.8 %dynamic_slice.6 = s32[256]{0:T(256)S(1)} dynamic-slice(s32[1024]{0:T(1024)} %param.12, s32[]{:T(128)S(6)} %select_n.8), dynamic_slice_sizes={256} | dynamic-slice | bytes 2052 | tf_op jit(solution)/shard_map/dynamic_slice | solution.py:173
  10.9 1.3 %bitcast_select_fusion.rows_ref = s32[16,256]{1,0:T(8,128)} fusion(s32[1024,16]{0,1:T(8,128)} %param.11, s32[]{:T(128)S(6)} %select_n.8, s32[256]{0:T(256)S(1)} %dynamic_slice.6), kind=kLoop, calls=%fused_computation.28 | loop fusion | flops 8192 | bytes 33796 | tf_op jit(solution)/shard_map/jit(_where)/select_n | solution.py:174
  12.2 26.3 %shard_map.73 = f32[4,256]{1,0:T(4,128)} custom-call(f32[128,1024]{1,0:T(8,128)} %slice_add_fusion.vt_ref, s32[16,256]{1,0:T(8,128)} %bitcast_select_fusion.rows_ref, s32[32,128]{1,0:T(8,128)} %bitcast.43, f32[32,128]{1,0:T(8,128)} %bitcast.44), custom_call_target="tpu_custom_call" | custom-call | tf_op jit(solution)/shard_map/pallas_call | solution.py:129
  38.5 1.3 %copy.41 = f32[256,4]{0,1:T(4,128)} copy(f32[256,4]{0,1:T(4,128)} %bitcast.42) | data formatting | bytes 8192
  (3 shorter events, 0.0 us)
Async XLA Ops:
  0.0 8.9 %copy-start = (bf16[1024,128]{1,0:T(8,128)(2,1)S(1)}, bf16[1024,128]{1,0:T(8,128)(2,1)}, u32[]{:S(2)}) copy-start(bf16[1024,128]{1,0:T(8,128)(2,1)} %param.13) | copy-start | bytes 786436

commit v6 on v5

--- a/solution.py
+++ b/solution.py
@@ -29,6 +29,21 @@
     step = 2.0 * math.pi / K
     scale = 1.0 / math.sqrt(K)
     norm_axle = 1.0 / math.sqrt(axles)
+    group = 8
+    groups = wave_count // group
+
+    def turns(m_first, station):
+        v_col = lax.broadcasted_iota(jnp.int32, (group, 1), 0)
+        coarse = (((m_first + group * v_col) * station) & (K - 1)).astype(jnp.float32) * step
+        fine = ((v_col * station) & (K - 1)).astype(jnp.float32) * step
+        c_coarse, s_coarse = jnp.cos(coarse), jnp.sin(coarse)
+        c_fine, s_fine = jnp.cos(fine), jnp.sin(fine)
+        blocks = []
+        for u in range(groups):
+            cu = c_coarse[u : u + 1, :]
+            su = s_coarse[u : u + 1, :]
+            blocks.append((cu * c_fine - su * s_fine, su * c_fine + cu * s_fine))
+        return blocks
 
     def kernel(vt_ref, rows_ref, pos_ref, load_ref, out_ref,
                recv_v, send_r, recv_r, v_send, v_recv, r_send, r_recv):
@@ -40,19 +55,21 @@
         for k in range(1, n_wave):
             pl.semaphore_signal(barrier, inc=1, device_id={"wave": lax.rem(me_w + k, n_wave)}, device_id_type=mesh_id)
 
-        m_col = me_w * wave_count + lax.broadcasted_iota(jnp.int32, (wave_count, 1), 0)
-        w_re = jnp.zeros((wave_count, own), jnp.float32)
-        w_im = jnp.zeros((wave_count, own), jnp.float32)
+        m_first = me_w * wave_count
         count = jnp.zeros((1, own), jnp.float32)
+        w_re = [jnp.zeros((group, own), jnp.float32) for _ in range(groups)]
+        w_im = [jnp.zeros((group, own), jnp.float32) for _ in range(groups)]
         for s in range(slots):
             station = rows_ref[s : s + 1, :]
-            angle = ((m_col * station) & (K - 1)).astype(jnp.float32) * step
-            t_re = (jnp.cos(angle) * scale).astype(jnp.bfloat16).astype(jnp.float32)
-            t_im = (-jnp.sin(angle) * scale).astype(jnp.bfloat16).astype(jnp.float32)
             used = jnp.where(station >= 0, 1.0, 0.0)
             count = count + used
-            w_re = w_re + used * t_re
-            w_im = w_im + used * t_im
+            for u, (c, sn) in enumerate(turns(m_first, station)):
+                t_re = (c * scale).astype(jnp.bfloat16).astype(jnp.float32)
+                t_im = (-sn * scale).astype(jnp.bfloat16).astype(jnp.float32)
+                w_re[u] = w_re[u] + used * t_re
+                w_im[u] = w_im[u] + used * t_im
+        w_re = jnp.concatenate(w_re, axis=0)
+        w_im = jnp.concatenate(w_im, axis=0)
 
         pl.semaphore_wait(barrier, n_dof - 1 + n_wave - 1)
         v_copies = []
@@ -69,13 +86,15 @@
             copy.start()
             v_copies.append(copy)
 
-        p_re = jnp.zeros((wave_count, cases), jnp.float32)
-        p_im = jnp.zeros((wave_count, cases), jnp.float32)
+        p_re = [jnp.zeros((group, cases), jnp.float32) for _ in range(groups)]
+        p_im = [jnp.zeros((group, cases), jnp.float32) for _ in range(groups)]
         for a in range(axles):
-            angle = ((m_col * pos_ref[a : a + 1, :]) & (K - 1)).astype(jnp.float32) * step
             load = load_ref[a : a + 1, :]
-            p_re = p_re + load * jnp.cos(angle)
-            p_im = p_im + load * jnp.sin(angle)
+            for u, (c, sn) in enumerate(turns(m_first, pos_ref[a : a + 1, :])):
+                p_re[u] = p_re[u] + load * c
+                p_im[u] = p_im[u] + load * sn
+        p_re = jnp.concatenate(p_re, axis=0)
+        p_im = jnp.concatenate(p_im, axis=0)
         phase = jnp.concatenate([p_re * norm_axle, -p_im * norm_axle], axis=0)
 
         row = lax.broadcasted_iota(jnp.int32, (n_wave * pad, cases), 0)

time: 40 us -> 37.9 us (0.948)
  Pallas kernels: 26.3 us -> 24.2 us
    pallas_call x1, Pallas kernels: 26.3 us -> 24.2 us  [exchange(): pl.pallas_call(kernel, out_shape=jax.ShapeDtypeStruct((per_wave, own), jn...]
where the time goes in v6:
time: 37.9 us; the launch traced here: 37.7 us
  Pallas kernels  24.2 us (64%)
  matrix products  7.42 us (20%)
  local copies, waits for them, and re-layouts  3.33 us (9%)
  other arithmetic  2.64 us (7%)
    pallas_call x1, Pallas kernels, exchange(): pl.pallas_call(kernel, out_shape=jax.ShapeDtypeStruct((per_wave, own), jn...  24.2 us
    dot_general x1, matrix products, body(): jnp.einsum('mkj,gmji->gmki', lhs, green, preferred_element_type=jnp.float32)  7.12 us
    select_n x1, other arithmetic, body(): jnp.where(jnp.arange(slot_count, dtype=jnp.int32)[:, None] < counts_own[N...  1.32 us
    unnamed x3, local copies, waits for them, and re-layouts  1.27 us
    slice x1, local copies, waits for them, and re-layouts, body(): re_hi, re_lo = split_bf16(rough[0])  1.03 us
    add x1, other arithmetic, body(): vt_part = both[:2 * wave_count] + both[2 * wave_count:]  0.86 us
    dynamic_slice x1, local copies, waits for them, and re-layouts, body(): counts_own = lax.dynamic_slice_in_dim(counts, first, own_buildings, 0)  0.76 us

profile of v6, /device:TPU:1, one launch (start us, length us, event | category | flops | bytes accessed | tf_op | source)
XLA Modules:
  0.0 37.7 jit_solution(12619551747759795499)
XLA Ops:
  0.0 0.0 copy-start
  0.0 1.0 %fusion.22 = (f32[1,64,512]{2,1,0:T(8,128)S(1)}, f32[1,64,512]{2,1,0:T(8,128)S(1)}) fusion(f32[2,64,512]{2,1,0:T(8,128)} %param.8), kind=kLoop, calls=%fused_computation.33 | loop fusion | bytes 524288 | tf_op jit(solution)/shard_map/slice | solution.py:175
  1.0 0.3 fusion.11
  1.3 0.3 subtract_convert_fusion
  1.6 7.1 %fusion.2 = f32[2,64,4,128]{3,2,0,1:T(4,128)S(1)} fusion(bf16[2,64,512,128]{3,2,1,0:T(8,128)(2,1)} %param.7, bf16[64,1,512]{2,1,0:T(2,128)(2,1)S(1)} %get-tuple-element.12, bf16[64,1,512]{2,1,0:T(2,128)(2,1)S(1)} %get-tuple-element.15, bf16[64,1,512]{2,1,0:T(2,128)(2,1)S(1)} %get-tuple-element.13, bf16[64,1,512]{2,1,0:T(2,128)(2,1)S(1)} %get-tuple-element.14), kind=kOutput, calls=%fused_computation.2 | convolution fusion | flops 68157440 | bytes 17301504 | tf_op jit(solution)/shard_map/mkj,gmji->gmki/dot_general | solution.py:178
  8.7 0.2 fusion.21
  8.9 0.0 copy-done
  8.9 0.3 fusion.13
  9.2 0.9 %slice_add_fusion.vt_ref = f32[128,1024]{1,0:T(8,128)} fusion(f32[256,1024]{1,0:T(8,128)S(1)} %fusion.13), kind=kLoop, calls=%fused_computation.3 | loop fusion | flops 131072 | bytes 1572864 | tf_op jit(solution)/shard_map/add | solution.py:188
  10.1 0.8 %dynamic_slice.6 = s32[256]{0:T(256)S(1)} dynamic-slice(s32[1024]{0:T(1024)} %param.12, s32[]{:T(128)S(6)} %select_n.8), dynamic_slice_sizes={256} | dynamic-slice | bytes 2052 | tf_op jit(solution)/shard_map/dynamic_slice | solution.py:192
  10.9 1.3 %bitcast_select_fusion.rows_ref = s32[16,256]{1,0:T(8,128)} fusion(s32[1024,16]{0,1:T(8,128)} %param.11, s32[]{:T(128)S(6)} %select_n.8, s32[256]{0:T(256)S(1)} %dynamic_slice.6), kind=kLoop, calls=%fused_computation.28 | loop fusion | flops 8192 | bytes 33796 | tf_op jit(solution)/shard_map/jit(_where)/select_n | solution.py:193
  12.2 24.2 %shard_map.73 = f32[4,256]{1,0:T(4,128)} custom-call(f32[128,1024]{1,0:T(8,128)} %slice_add_fusion.vt_ref, s32[16,256]{1,0:T(8,128)} %bitcast_select_fusion.rows_ref, s32[32,128]{1,0:T(8,128)} %bitcast.43, f32[32,128]{1,0:T(8,128)} %bitcast.44), custom_call_target="tpu_custom_call" | custom-call | tf_op jit(solution)/shard_map/pallas_call | solution.py:148
  36.4 1.3 %copy.41 = f32[256,4]{0,1:T(4,128)} copy(f32[256,4]{0,1:T(4,128)} %bitcast.42) | data formatting | bytes 8192
  (3 shorter events, 0.0 us)
Async XLA Ops:
  0.0 8.9 %copy-start = (bf16[1024,128]{1,0:T(8,128)(2,1)S(1)}, bf16[1024,128]{1,0:T(8,128)(2,1)}, u32[]{:S(2)}) copy-start(bf16[1024,128]{1,0:T(8,128)(2,1)} %param.13) | copy-start | bytes 786436

commit v7 on v6

--- a/solution.py
+++ b/solution.py
@@ -16,7 +16,7 @@
     return hi, lo
 
 
-def exchange(vt, rows_t, pos_t, load_t, wave_count):
+def exchange(vt, rows_t, counts_row, pos_t, load_t, wave_count):
     n_dof = lax.axis_size("dof")
     n_wave = lax.axis_size("wave")
     modes = vt.shape[0]
@@ -45,7 +45,7 @@
             blocks.append((cu * c_fine - su * s_fine, su * c_fine + cu * s_fine))
         return blocks
 
-    def kernel(vt_ref, rows_ref, pos_ref, load_ref, out_ref,
+    def kernel(vt_ref, rows_ref, counts_ref, pos_ref, load_ref, out_ref,
                recv_v, send_r, recv_r, v_send, v_recv, r_send, r_recv):
         me_d = lax.axis_index("dof")
         me_w = lax.axis_index("wave")
@@ -54,22 +54,6 @@
             pl.semaphore_signal(barrier, inc=1, device_id={"dof": lax.rem(me_d + k, n_dof)}, device_id_type=mesh_id)
         for k in range(1, n_wave):
             pl.semaphore_signal(barrier, inc=1, device_id={"wave": lax.rem(me_w + k, n_wave)}, device_id_type=mesh_id)
-
-        m_first = me_w * wave_count
-        count = jnp.zeros((1, own), jnp.float32)
-        w_re = [jnp.zeros((group, own), jnp.float32) for _ in range(groups)]
-        w_im = [jnp.zeros((group, own), jnp.float32) for _ in range(groups)]
-        for s in range(slots):
-            station = rows_ref[s : s + 1, :]
-            used = jnp.where(station >= 0, 1.0, 0.0)
-            count = count + used
-            for u, (c, sn) in enumerate(turns(m_first, station)):
-                t_re = (c * scale).astype(jnp.bfloat16).astype(jnp.float32)
-                t_im = (-sn * scale).astype(jnp.bfloat16).astype(jnp.float32)
-                w_re[u] = w_re[u] + used * t_re
-                w_im[u] = w_im[u] + used * t_im
-        w_re = jnp.concatenate(w_re, axis=0)
-        w_im = jnp.concatenate(w_im, axis=0)
 
         pl.semaphore_wait(barrier, n_dof - 1 + n_wave - 1)
         v_copies = []
@@ -85,6 +69,22 @@
             )
             copy.start()
             v_copies.append(copy)
+
+        m_first = me_w * wave_count
+        mine = pl.ds(pl.multiple_of(me_d * own, own), own)
+        count = counts_ref[:, mine]
+        w_re = [jnp.zeros((group, own), jnp.float32) for _ in range(groups)]
+        w_im = [jnp.zeros((group, own), jnp.float32) for _ in range(groups)]
+        for s in range(slots):
+            station = rows_ref[s : s + 1, mine]
+            used = jnp.where(count > s, 1.0, 0.0)
+            for u, (c, sn) in enumerate(turns(m_first, station)):
+                t_re = (c * scale).astype(jnp.bfloat16).astype(jnp.float32)
+                t_im = (-sn * scale).astype(jnp.bfloat16).astype(jnp.float32)
+                w_re[u] = w_re[u] + used * t_re
+                w_im[u] = w_im[u] + used * t_im
+        w_re = jnp.concatenate(w_re, axis=0)
+        w_im = jnp.concatenate(w_im, axis=0)
 
         p_re = [jnp.zeros((group, cases), jnp.float32) for _ in range(groups)]
         p_im = [jnp.zeros((group, cases), jnp.float32) for _ in range(groups)]
@@ -143,12 +143,12 @@
         result = result[0:per_wave]
         for k in range(n_wave - 1):
             result = result + recv_r[k, 0:per_wave]
-        out_ref[...] = result / count
+        out_ref[...] = result / count.astype(jnp.float32)
 
     return pl.pallas_call(
         kernel,
         out_shape=jax.ShapeDtypeStruct((per_wave, own), jnp.float32),
-        in_specs=[pl.BlockSpec(memory_space=pltpu.VMEM)] * 4,
+        in_specs=[pl.BlockSpec(memory_space=pltpu.VMEM)] * 5,
         out_specs=pl.BlockSpec(memory_space=pltpu.VMEM),
         scratch_shapes=[
             pltpu.VMEM((n_dof - 1, modes, own), jnp.float32),
@@ -160,7 +160,7 @@
             pltpu.SemaphoreType.DMA((n_wave - 1,)),
         ],
         compiler_params=pltpu.CompilerParams(collective_id=0, has_side_effects=True),
-    )(vt, rows_t, pos_t, load_t)
+    )(vt, rows_t, counts_row, pos_t, load_t)
 
 
 def body(green, rough, axle_pos, axle_load, rows, counts, coupling):
@@ -182,18 +182,11 @@
     gim_rim = prod[1, :, 2] + prod[1, :, 3]
     h_cat = jnp.concatenate([gre_rre - gim_rim, gre_rim + gim_rre], axis=0)
 
-    h_hi, h_lo = split_bf16(h_cat)
-    rhs = jnp.concatenate([h_hi, h_lo], axis=0)
-    both = jnp.einsum("ni,bi->nb", rhs, coupling, preferred_element_type=jnp.float32)
-    vt_part = both[: 2 * wave_count] + both[2 * wave_count :]
-
-    first = lax.axis_index("dof") * own_buildings
-    rows_own = lax.dynamic_slice_in_dim(rows, first, own_buildings, 0)
-    counts_own = lax.dynamic_slice_in_dim(counts, first, own_buildings, 0)
-    rows_used = jnp.where(
-        jnp.arange(slot_count, dtype=jnp.int32)[:, None] < counts_own[None, :], rows_own.T, -1
+    vt_part = lax.dot_general(
+        h_cat, coupling, (((1,), (1,)), ((), ())),
+        precision=lax.Precision.HIGHEST, preferred_element_type=jnp.float32,
     )
-    return exchange(vt_part, rows_used, axle_pos.T, axle_load.T, wave_count).T
+    return exchange(vt_part, rows.T, counts.reshape(1, -1), axle_pos.T, axle_load.T, wave_count).T
 
 
 def solution(mesh):

time: 37.9 us -> 35.8 us (0.945)
  other arithmetic: 2.64 us -> 0.44 us
  matrix products: 7.42 us -> 8.29 us
  local copies, waits for them, and re-layouts: 3.33 us -> 2.57 us
    select_n x1 -> x0, other arithmetic: 1.32 us -> none  [body(): jnp.where(jnp.arange(slot_count, dtype=jnp.int32)[:, None] < counts_own[N...]
    dot_general x1, matrix products: 0.3 us -> 1.17 us  [body(): lax.dot_general(h_cat, coupling, (((1,), (1,)), ((), ())), precision=lax....]
    add x1 -> x0, other arithmetic: 0.86 us -> none  [body(): vt_part = both[:2 * wave_count] + both[2 * wave_count:]]
    dynamic_slice x1 -> x0, local copies, waits for them, and re-layouts: 0.76 us -> none  [body(): counts_own = lax.dynamic_slice_in_dim(counts, first, own_buildings, 0)]
where the time goes in v7:
time: 35.8 us; the launch traced here: 35.7 us
  Pallas kernels  24.3 us (68%)
  matrix products  8.29 us (23%)
  local copies, waits for them, and re-layouts  2.57 us (7%)
  other arithmetic  0.44 us (1%)
    pallas_call x1, Pallas kernels, exchange(): pl.pallas_call(kernel, out_shape=jax.ShapeDtypeStruct((per_wave, own), jn...  24.3 us
    dot_general x1, matrix products, body(): jnp.einsum('mkj,gmji->gmki', lhs, green, preferred_element_type=jnp.float32)  7.12 us
    unnamed x3, local copies, waits for them, and re-layouts  1.27 us
    dot_general x1, matrix products, body(): lax.dot_general(h_cat, coupling, (((1,), (1,)), ((), ())), precision=lax....  1.17 us
    slice x1, local copies, waits for them, and re-layouts, body(): re_hi, re_lo = split_bf16(rough[0])  1.03 us

profile of v7, /device:TPU:1, one launch (start us, length us, event | category | flops | bytes accessed | tf_op | source)
XLA Modules:
  0.0 35.7 jit_solution(2491183896020752930)
XLA Ops:
  0.0 0.0 copy-start
  0.0 1.0 %fusion.21 = (f32[1,64,512]{2,1,0:T(8,128)S(1)}, f32[1,64,512]{2,1,0:T(8,128)S(1)}) fusion(f32[2,64,512]{2,1,0:T(8,128)} %param.8), kind=kLoop, calls=%fused_computation.27 | loop fusion | bytes 524288 | tf_op jit(solution)/shard_map/slice | solution.py:175
  1.0 0.3 subtract_convert_fusion
  1.3 0.3 fusion.11
  1.6 7.1 %fusion.2 = f32[2,64,4,128]{3,2,0,1:T(4,128)S(1)} fusion(bf16[2,64,512,128]{3,2,1,0:T(8,128)(2,1)} %param.7, bf16[64,1,512]{2,1,0:T(2,128)(2,1)S(1)} %get-tuple-element.12, bf16[64,1,512]{2,1,0:T(2,128)(2,1)S(1)} %get-tuple-element.15, bf16[64,1,512]{2,1,0:T(2,128)(2,1)S(1)} %get-tuple-element.13, bf16[64,1,512]{2,1,0:T(2,128)(2,1)S(1)} %get-tuple-element.14), kind=kOutput, calls=%fused_computation.2 | convolution fusion | flops 68157440 | bytes 17301504 | tf_op jit(solution)/shard_map/mkj,gmji->gmki/dot_general | solution.py:178
  8.7 0.2 fusion.20
  8.9 0.0 copy-done
  8.9 1.2 %fusion.13.vt_ref = f32[128,1024]{1,0:T(8,128)} fusion(bf16[1024,128]{1,0:T(8,128)(2,1)S(1)} %copy-done, f32[64,128]{1,0:T(8,128)S(1)} %bitcast.40, f32[64,128]{1,0:T(8,128)S(1)} %subtract_bitcast_fusion), kind=kOutput, calls=%fused_computation.16 | convolution fusion | flops 201342976 | bytes 851968 | tf_op jit(solution)/shard_map/dot_general | solution.py:185
  10.1 24.3 %shard_map.73 = f32[4,256]{1,0:T(4,128)} custom-call(f32[128,1024]{1,0:T(8,128)} %fusion.13.vt_ref, s32[16,1024]{1,0:T(8,128)} %bitcast.41, s32[1,1024]{1,0:T(1,128)} %bitcast.45, s32[32,128]{1,0:T(8,128)} %bitcast.43, f32[32,128]{1,0:T(8,128)} %bitcast.44), custom_call_target="tpu_custom_call" | custom-call | tf_op jit(solution)/shard_map/pallas_call | solution.py:148
  34.4 1.3 %copy.41 = f32[256,4]{0,1:T(4,128)} copy(f32[256,4]{0,1:T(4,128)} %bitcast.42) | data formatting | bytes 8192
  (1 shorter events, 0.0 us)
Async XLA Ops:
  0.0 8.9 %copy-start = (bf16[1024,128]{1,0:T(8,128)(2,1)S(1)}, bf16[1024,128]{1,0:T(8,128)(2,1)}, u32[]{:S(2)}) copy-start(bf16[1024,128]{1,0:T(8,128)(2,1)} %param.13) | copy-start | bytes 786436

commit v8 on v7

--- a/solution.py
+++ b/solution.py
@@ -16,11 +16,16 @@
     return hi, lo
 
 
-def exchange(vt, rows_t, counts_row, pos_t, load_t, wave_count):
+def exchange(green, lhs, coupling, rows_t, counts_row, pos_t, load_t):
     n_dof = lax.axis_size("dof")
     n_wave = lax.axis_size("wave")
-    modes = vt.shape[0]
-    own = vt.shape[1] // n_dof
+    wave_count = green.shape[1]
+    modes = 2 * wave_count
+    dofs = green.shape[3]
+    forcing = green.shape[2]
+    own = coupling.shape[0] // n_dof
+    block = 8
+    blocks = wave_count // block
     slots, cases = rows_t.shape[0], pos_t.shape[1]
     axles = pos_t.shape[0]
     per_wave = cases // n_wave
@@ -45,8 +50,9 @@
             blocks.append((cu * c_fine - su * s_fine, su * c_fine + cu * s_fine))
         return blocks
 
-    def kernel(vt_ref, rows_ref, counts_ref, pos_ref, load_ref, out_ref,
-               recv_v, send_r, recv_r, v_send, v_recv, r_send, r_recv):
+    def kernel(green_hbm, lhs_ref, cpl_ref, rows_ref, counts_ref, pos_ref, load_ref, out_ref,
+               gbuf, gsem, raw, h_send, recv_h, recv_c, send_r, recv_r,
+               h_sems, c_sems, r_send, r_recv):
         me_d = lax.axis_index("dof")
         me_w = lax.axis_index("wave")
         barrier = pltpu.get_barrier_semaphore()
@@ -55,20 +61,55 @@
         for k in range(1, n_wave):
             pl.semaphore_signal(barrier, inc=1, device_id={"wave": lax.rem(me_w + k, n_wave)}, device_id_type=mesh_id)
 
+        def fetch(t, slot):
+            pltpu.make_async_copy(
+                green_hbm.at[:, pl.ds(pl.multiple_of(t * block, block), block)], gbuf.at[slot], gsem.at[slot]
+            ).start()
+
+        fetch(0, 0)
         pl.semaphore_wait(barrier, n_dof - 1 + n_wave - 1)
-        v_copies = []
+
+        def remote(src_ref, dst_ref, sems, k, peer):
+            return pltpu.make_async_remote_copy(
+                src_ref=src_ref, dst_ref=dst_ref, send_sem=sems.at[0, k - 1], recv_sem=sems.at[1, k - 1],
+                device_id={"dof": peer}, device_id_type=mesh_id,
+            )
+
+        c_copies = []
         for k in range(1, n_dof):
             peer = lax.rem(me_d + k, n_dof)
-            copy = pltpu.make_async_remote_copy(
-                src_ref=vt_ref.at[:, pl.ds(pl.multiple_of(peer * own, own), own)],
-                dst_ref=recv_v.at[k - 1],
-                send_sem=v_send.at[k - 1],
-                recv_sem=v_recv.at[k - 1],
-                device_id={"dof": peer},
-                device_id_type=mesh_id,
-            )
+            copy = remote(cpl_ref.at[pl.ds(pl.multiple_of(peer * own, own), own)], recv_c.at[k - 1], c_sems, k, peer)
             copy.start()
-            v_copies.append(copy)
+            c_copies.append(copy)
+
+        def matvec(t, carry):
+            slot = lax.rem(t, 2)
+            pltpu.make_async_copy(green_hbm.at[:, pl.ds(0, block)], gbuf.at[slot], gsem.at[slot]).wait()
+
+            @pl.when(t + 1 < blocks)
+            def _():
+                fetch(t + 1, 1 - slot)
+
+            first = pl.multiple_of(t * block, block)
+            for mm in range(block):
+                l = lhs_ref[first + mm]
+                for g in range(2):
+                    raw[g, first + mm] = jnp.dot(l, gbuf[slot, g, mm], preferred_element_type=jnp.float32)
+            return carry
+
+        lax.fori_loop(0, blocks, matvec, 0)
+        gre_rre = raw[0, :, 0, :] + raw[0, :, 1, :]
+        gre_rim = raw[0, :, 2, :] + raw[0, :, 3, :]
+        gim_rre = raw[1, :, 0, :] + raw[1, :, 1, :]
+        gim_rim = raw[1, :, 2, :] + raw[1, :, 3, :]
+        h_send[0:wave_count, :] = gre_rre - gim_rim
+        h_send[wave_count:modes, :] = gre_rim + gim_rre
+        h_copies = []
+        for k in range(1, n_dof):
+            peer = lax.rem(me_d + k, n_dof)
+            copy = remote(h_send, recv_h.at[k - 1], h_sems, k, peer)
+            copy.start()
+            h_copies.append(copy)
 
         m_first = me_w * wave_count
         mine = pl.ds(pl.multiple_of(me_d * own, own), own)
@@ -107,11 +148,19 @@
         pt_hi = lax.dot_general(spread, ph_hi, dims, preferred_element_type=jnp.float32).astype(jnp.bfloat16)
         pt_lo = lax.dot_general(spread, ph_lo, dims, preferred_element_type=jnp.float32).astype(jnp.bfloat16)
 
-        for copy in v_copies:
+        mine_rows = pl.ds(pl.multiple_of(me_d * own, own), own)
+        dims_t = (((1,), (1,)), ((), ()))
+
+        def v_term(h, c):
+            h_hi, h_lo = split_bf16(h)
+            return (lax.dot_general(h_hi, c, dims_t, preferred_element_type=jnp.float32)
+                    + lax.dot_general(h_lo, c, dims_t, preferred_element_type=jnp.float32))
+
+        total = v_term(h_send[...], cpl_ref[mine_rows, :])
+        for copy in c_copies + h_copies:
             copy.wait()
-        total = vt_ref[:, pl.ds(pl.multiple_of(me_d * own, own), own)]
         for k in range(n_dof - 1):
-            total = total + recv_v[k]
+            total = total + v_term(recv_h[k], recv_c[k])
         v_re = total[0:wave_count]
         v_im = total[wave_count : 2 * wave_count]
         ab = jnp.concatenate([w_re * v_re + w_im * v_im, w_im * v_re - w_re * v_im], axis=0)
@@ -148,19 +197,24 @@
     return pl.pallas_call(
         kernel,
         out_shape=jax.ShapeDtypeStruct((per_wave, own), jnp.float32),
-        in_specs=[pl.BlockSpec(memory_space=pltpu.VMEM)] * 5,
+        in_specs=[pl.BlockSpec(memory_space=pl.ANY)] + [pl.BlockSpec(memory_space=pltpu.VMEM)] * 6,
         out_specs=pl.BlockSpec(memory_space=pltpu.VMEM),
         scratch_shapes=[
-            pltpu.VMEM((n_dof - 1, modes, own), jnp.float32),
+            pltpu.VMEM((2, 2, block, forcing, dofs), green.dtype),
+            pltpu.SemaphoreType.DMA((2,)),
+            pltpu.VMEM((2, wave_count, 8, dofs), jnp.float32),
+            pltpu.VMEM((modes, dofs), jnp.float32),
+            pltpu.VMEM((n_dof - 1, modes, dofs), jnp.float32),
+            pltpu.VMEM((n_dof - 1, own, dofs), coupling.dtype),
             pltpu.VMEM((n_wave, pad, own), jnp.float32),
             pltpu.VMEM((n_wave - 1, pad, own), jnp.float32),
-            pltpu.SemaphoreType.DMA((n_dof - 1,)),
-            pltpu.SemaphoreType.DMA((n_dof - 1,)),
+            pltpu.SemaphoreType.DMA((2, n_dof - 1)),
+            pltpu.SemaphoreType.DMA((2, n_dof - 1)),
             pltpu.SemaphoreType.DMA((n_wave - 1,)),
             pltpu.SemaphoreType.DMA((n_wave - 1,)),
         ],
         compiler_params=pltpu.CompilerParams(collective_id=0, has_side_effects=True),
-    )(vt, rows_t, counts_row, pos_t, load_t)
+    )(green, lhs, coupling, rows_t, counts_row, pos_t, load_t)
 
 
 def body(green, rough, axle_pos, axle_load, rows, counts, coupling):
@@ -174,19 +228,9 @@
 
     re_hi, re_lo = split_bf16(rough[0])
     im_hi, im_lo = split_bf16(rough[1])
-    lhs = jnp.stack([re_hi, re_lo, im_hi, im_lo], axis=1)
-    prod = jnp.einsum("mkj,gmji->gmki", lhs, green, preferred_element_type=jnp.float32)
-    gre_rre = prod[0, :, 0] + prod[0, :, 1]
-    gre_rim = prod[0, :, 2] + prod[0, :, 3]
-    gim_rre = prod[1, :, 0] + prod[1, :, 1]
-    gim_rim = prod[1, :, 2] + prod[1, :, 3]
-    h_cat = jnp.concatenate([gre_rre - gim_rim, gre_rim + gim_rre], axis=0)
-
-    vt_part = lax.dot_general(
-        h_cat, coupling, (((1,), (1,)), ((), ())),
-        precision=lax.Precision.HIGHEST, preferred_element_type=jnp.float32,
-    )
-    return exchange(vt_part, rows.T, counts.reshape(1, -1), axle_pos.T, axle_load.T, wave_count).T
+    zero = jnp.zeros_like(re_hi)
+    lhs = jnp.stack([re_hi, re_lo, im_hi, im_lo, zero, zero, zero, zero], axis=1)
+    return exchange(green, lhs, coupling, rows.T, counts.reshape(1, -1), axle_pos.T, axle_load.T).T
 
 
 def solution(mesh):

time: 35.8 us -> 39 us (1.089)
  Pallas kernels: 24.3 us -> 33.7 us
  matrix products: 8.29 us -> 0 us
  local copies, waits for them, and re-layouts: 2.57 us -> 4.61 us
    pallas_call x1, Pallas kernels: 24.3 us -> 33.7 us  [exchange(): pl.pallas_call(kernel, out_shape=jax.ShapeDtypeStruct((per_wave, own), jn...]
    dot_general x2 -> x0, matrix products: 8.29 us -> none  [the longest x1 7.12 us: body(): jnp.einsum('mkj,gmji->gmki', lhs, green, preferred_element_type=jnp.float32)]
    another operation x0 -> x2, local copies, waits for them, and re-layouts: none -> 2.09 us  [body(): jnp.stack([re_hi, re_lo, im_hi, im_lo, zero, zero, zero, zero], axis=1)]
    unnamed x3 -> x1, local copies, waits for them, and re-layouts: 1.27 us -> 1.27 us
where the time goes in v8:
time: 39 us; the launch traced here: 38.6 us
  Pallas kernels  33.7 us (86%)
  local copies, waits for them, and re-layouts  4.61 us (12%)
    pallas_call x1, Pallas kernels, exchange(): pl.pallas_call(kernel, out_shape=jax.ShapeDtypeStruct((per_wave, own), jn...  33.7 us
    another operation x2, local copies, waits for them, and re-layouts, body(): jnp.stack([re_hi, re_lo, im_hi, im_lo, zero, zero, zero, zero], axis=1)  2.09 us
    unnamed x1, local copies, waits for them, and re-layouts  1.27 us
    slice x1, local copies, waits for them, and re-layouts, body(): im_hi, im_lo = split_bf16(rough[1])  0.99 us

profile of v8, /device:TPU:1, one launch (start us, length us, event | category | flops | bytes accessed | tf_op | source)
XLA Modules:
  0.0 38.6 jit_solution(5119504915228578745)
XLA Ops:
  0.0 1.0 %fusion.2 = (f32[1,64,512]{2,1,0:T(8,128)S(1)}, f32[1,64,512]{2,1,0:T(8,128)S(1)}) fusion(f32[2,64,512]{2,1,0:T(8,128)} %param.8), kind=kLoop, calls=%fused_computation.6 | loop fusion | bytes 524288 | tf_op jit(solution)/shard_map/slice | solution.py:230
  1.0 0.3 subtract_convert_fusion
  1.3 0.3 fusion
  1.5 0.1 stack.4
  1.6 2.0 %stack.5.lhs_ref = bf16[64,8,512]{2,1,0:T(8,128)(2,1)} concatenate(bf16[64,1,512]{2,1,0:T(2,128)(2,1)S(1)} %get-tuple-element.9, bf16[64,1,512]{2,1,0:T(2,128)(2,1)S(1)} %get-tuple-element.8, bf16[64,1,512]{2,1,0:T(2,128)(2,1)S(1)} %get-tuple-element.10, bf16[64,1,512]{2,1,0:T(2,128)(2,1)S(1)} %get-tuple-element.7, bf16[64,4,512]{2,1,0:T(4,128)(2,1)S(1)} %stack.4), dimensions={1} | concatenate | bytes 1048576 | tf_op jit(solution)/shard_map/stack | solution.py:232
  3.6 33.7 %shard_map.73 = f32[4,256]{1,0:T(4,128)} custom-call(bf16[2,64,512,128]{3,2,1,0:T(8,128)(2,1)} %green_hbm.1, bf16[64,8,512]{2,1,0:T(8,128)(2,1)} %stack.5.lhs_ref, bf16[1024,128]{1,0:T(8,128)(2,1)} %cpl_ref.1, s32[16,1024]{1,0:T(8,128)} %bitcast.21, s32[1,1024]{1,0:T(1,128)} %bitcast.25, s32[32,128]{1,0:T(8,128)} %bitcast.22, f32[32,128]{1,0:T(8,128)} %bitcast.23), custom_call_target="tpu_custom_call" | custom-call | tf_op jit(solution)/shard_map/pallas_call | solution.py:197
  37.3 1.3 %copy.27 = f32[256,4]{0,1:T(4,128)} copy(f32[256,4]{0,1:T(4,128)} %bitcast.24) | data formatting | bytes 8192

commit v9 on v7

--- a/solution.py
+++ b/solution.py
@@ -16,7 +16,7 @@
     return hi, lo
 
 
-def exchange(vt, rows_t, counts_row, pos_t, load_t, wave_count):
+def exchange(vt, vt_link, rows_t, counts_row, pos_t, load_t, wave_count):
     n_dof = lax.axis_size("dof")
     n_wave = lax.axis_size("wave")
     modes = vt.shape[0]
@@ -45,7 +45,7 @@
             blocks.append((cu * c_fine - su * s_fine, su * c_fine + cu * s_fine))
         return blocks
 
-    def kernel(vt_ref, rows_ref, counts_ref, pos_ref, load_ref, out_ref,
+    def kernel(vt_ref, link_ref, rows_ref, counts_ref, pos_ref, load_ref, out_ref,
                recv_v, send_r, recv_r, v_send, v_recv, r_send, r_recv):
         me_d = lax.axis_index("dof")
         me_w = lax.axis_index("wave")
@@ -60,7 +60,7 @@
         for k in range(1, n_dof):
             peer = lax.rem(me_d + k, n_dof)
             copy = pltpu.make_async_remote_copy(
-                src_ref=vt_ref.at[:, pl.ds(pl.multiple_of(peer * own, own), own)],
+                src_ref=link_ref.at[:, pl.ds(pl.multiple_of(peer * own, own), own)],
                 dst_ref=recv_v.at[k - 1],
                 send_sem=v_send.at[k - 1],
                 recv_sem=v_recv.at[k - 1],
@@ -111,7 +111,7 @@
             copy.wait()
         total = vt_ref[:, pl.ds(pl.multiple_of(me_d * own, own), own)]
         for k in range(n_dof - 1):
-            total = total + recv_v[k]
+            total = total + recv_v[k].astype(jnp.float32)
         v_re = total[0:wave_count]
         v_im = total[wave_count : 2 * wave_count]
         ab = jnp.concatenate([w_re * v_re + w_im * v_im, w_im * v_re - w_re * v_im], axis=0)
@@ -148,10 +148,10 @@
     return pl.pallas_call(
         kernel,
         out_shape=jax.ShapeDtypeStruct((per_wave, own), jnp.float32),
-        in_specs=[pl.BlockSpec(memory_space=pltpu.VMEM)] * 5,
+        in_specs=[pl.BlockSpec(memory_space=pltpu.VMEM)] * 6,
         out_specs=pl.BlockSpec(memory_space=pltpu.VMEM),
         scratch_shapes=[
-            pltpu.VMEM((n_dof - 1, modes, own), jnp.float32),
+            pltpu.VMEM((n_dof - 1, modes, own), vt_link.dtype),
             pltpu.VMEM((n_wave, pad, own), jnp.float32),
             pltpu.VMEM((n_wave - 1, pad, own), jnp.float32),
             pltpu.SemaphoreType.DMA((n_dof - 1,)),
@@ -160,7 +160,7 @@
             pltpu.SemaphoreType.DMA((n_wave - 1,)),
         ],
         compiler_params=pltpu.CompilerParams(collective_id=0, has_side_effects=True),
-    )(vt, rows_t, counts_row, pos_t, load_t)
+    )(vt, vt_link, rows_t, counts_row, pos_t, load_t)
 
 
 def body(green, rough, axle_pos, axle_load, rows, counts, coupling):
@@ -186,7 +186,7 @@
         h_cat, coupling, (((1,), (1,)), ((), ())),
         precision=lax.Precision.HIGHEST, preferred_element_type=jnp.float32,
     )
-    return exchange(vt_part, rows.T, counts.reshape(1, -1), axle_pos.T, axle_load.T, wave_count).T
+    return exchange(vt_part, vt_part.astype(jnp.bfloat16), rows.T, counts.reshape(1, -1), axle_pos.T, axle_load.T, wave_count).T
 
 
 def solution(mesh):

time: 35.8 us -> 33.2 us (0.927)
  Pallas kernels: 24.3 us -> 21.5 us
    pallas_call x1, Pallas kernels: 24.3 us -> 21.5 us  [exchange(): pl.pallas_call(kernel, out_shape=jax.ShapeDtypeStruct((per_wave, own), jn...]
where the time goes in v9:
time: 33.2 us; the launch traced here: 33 us
  Pallas kernels  21.5 us (65%)
  matrix products  8.39 us (25%)
  local copies, waits for them, and re-layouts  2.58 us (8%)
  other arithmetic  0.44 us (1%)
    pallas_call x1, Pallas kernels, exchange(): pl.pallas_call(kernel, out_shape=jax.ShapeDtypeStruct((per_wave, own), jn...  21.5 us
    dot_general x1, matrix products, body(): jnp.einsum('mkj,gmji->gmki', lhs, green, preferred_element_type=jnp.float32)  7.12 us
    unnamed x3, local copies, waits for them, and re-layouts  1.28 us
    dot_general x1, matrix products, body(): lax.dot_general(h_cat, coupling, (((1,), (1,)), ((), ())), precision=lax....  1.27 us
    slice x1, local copies, waits for them, and re-layouts, body(): re_hi, re_lo = split_bf16(rough[0])  1.03 us

profile of v9, /device:TPU:1, one launch (start us, length us, event | category | flops | bytes accessed | tf_op | source)
XLA Modules:
  0.0 33.0 jit_solution(2562751887808460653)
XLA Ops:
  0.0 0.0 copy-start
  0.0 1.0 %fusion.21 = (f32[1,64,512]{2,1,0:T(8,128)S(1)}, f32[1,64,512]{2,1,0:T(8,128)S(1)}) fusion(f32[2,64,512]{2,1,0:T(8,128)} %param.8), kind=kLoop, calls=%fused_computation.27 | loop fusion | bytes 524288 | tf_op jit(solution)/shard_map/slice | solution.py:175
  1.0 0.3 subtract_convert_fusion
  1.3 0.3 fusion.11
  1.6 7.1 %fusion.2 = f32[2,64,4,128]{3,2,0,1:T(4,128)S(1)} fusion(bf16[2,64,512,128]{3,2,1,0:T(8,128)(2,1)} %param.7, bf16[64,1,512]{2,1,0:T(2,128)(2,1)S(1)} %get-tuple-element.14, bf16[64,1,512]{2,1,0:T(2,128)(2,1)S(1)} %get-tuple-element.17, bf16[64,1,512]{2,1,0:T(2,128)(2,1)S(1)} %get-tuple-element.15, bf16[64,1,512]{2,1,0:T(2,128)(2,1)S(1)} %get-tuple-element.16), kind=kOutput, calls=%fused_computation.2 | convolution fusion | flops 68157440 | bytes 17301504 | tf_op jit(solution)/shard_map/mkj,gmji->gmki/dot_general | solution.py:178
  8.7 0.2 fusion.20
  8.9 0.0 copy-done
  8.9 1.3 %fusion.22 = (bf16[128,1024]{1,0:T(8,128)(2,1)}, f32[128,1024]{1,0:T(8,128)}) fusion(bf16[1024,128]{1,0:T(8,128)(2,1)S(1)} %copy-done, f32[64,128]{1,0:T(8,128)S(1)} %bitcast.36, f32[64,128]{1,0:T(8,128)S(1)} %subtract_bitcast_fusion), kind=kOutput, calls=%fused_computation.28 | convolution fusion | flops 201474048 | bytes 1114112 | tf_op jit(solution)/shard_map/dot_general | solution.py:185
  10.2 21.5 %shard_map.73 = f32[4,256]{1,0:T(4,128)} custom-call(f32[128,1024]{1,0:T(8,128)} %get-tuple-element.13.vt_ref, bf16[128,1024]{1,0:T(8,128)(2,1)} %get-tuple-element.12.link_ref, s32[16,1024]{1,0:T(8,128)} %bitcast.41, s32[1,1024]{1,0:T(1,128)} %bitcast.45, s32[32,128]{1,0:T(8,128)} %bitcast.42, f32[32,128]{1,0:T(8,128)} %bitcast.43), custom_call_target="tpu_custom_call" | custom-call | tf_op jit(solution)/shard_map/pallas_call | solution.py:148
  31.7 1.3 %copy.41 = f32[256,4]{0,1:T(4,128)} copy(f32[256,4]{0,1:T(4,128)} %bitcast.44) | data formatting | bytes 8192
  (1 shorter events, 0.0 us)
Async XLA Ops:
  0.0 8.9 %copy-start = (bf16[1024,128]{1,0:T(8,128)(2,1)S(1)}, bf16[1024,128]{1,0:T(8,128)(2,1)}, u32[]{:S(2)}) copy-start(bf16[1024,128]{1,0:T(8,128)(2,1)} %param.13) | copy-start | bytes 786436

commit v10 on v9

--- a/solution.py
+++ b/solution.py
@@ -16,11 +16,11 @@
     return hi, lo
 
 
-def exchange(vt, vt_link, rows_t, counts_row, pos_t, load_t, wave_count):
+def exchange(h_cat, coupling, rows_t, counts_row, pos_t, load_t, wave_count):
     n_dof = lax.axis_size("dof")
     n_wave = lax.axis_size("wave")
-    modes = vt.shape[0]
-    own = vt.shape[1] // n_dof
+    modes = h_cat.shape[0]
+    own = coupling.shape[0] // n_dof
     slots, cases = rows_t.shape[0], pos_t.shape[1]
     axles = pos_t.shape[0]
     per_wave = cases // n_wave
@@ -45,8 +45,8 @@
             blocks.append((cu * c_fine - su * s_fine, su * c_fine + cu * s_fine))
         return blocks
 
-    def kernel(vt_ref, link_ref, rows_ref, counts_ref, pos_ref, load_ref, out_ref,
-               recv_v, send_r, recv_r, v_send, v_recv, r_send, r_recv):
+    def kernel(h_ref, cpl_ref, rows_ref, counts_ref, pos_ref, load_ref, out_ref,
+               link_ref, recv_v, send_r, recv_r, v_send, v_recv, r_send, r_recv):
         me_d = lax.axis_index("dof")
         me_w = lax.axis_index("wave")
         barrier = pltpu.get_barrier_semaphore()
@@ -55,6 +55,16 @@
         for k in range(1, n_wave):
             pl.semaphore_signal(barrier, inc=1, device_id={"wave": lax.rem(me_w + k, n_wave)}, device_id_type=mesh_id)
 
+        h_hi, h_lo = split_bf16(h_ref[...])
+        dims_t = (((1,), (1,)), ((), ()))
+
+        def v_of(c):
+            return (lax.dot_general(h_hi, c, dims_t, preferred_element_type=jnp.float32)
+                    + lax.dot_general(h_lo, c, dims_t, preferred_element_type=jnp.float32))
+
+        link_ref[...] = v_of(cpl_ref[...]).astype(link_ref.dtype)
+        mine = pl.ds(pl.multiple_of(me_d * own, own), own)
+        total = v_of(cpl_ref[mine, :])
         pl.semaphore_wait(barrier, n_dof - 1 + n_wave - 1)
         v_copies = []
         for k in range(1, n_dof):
@@ -71,7 +81,6 @@
             v_copies.append(copy)
 
         m_first = me_w * wave_count
-        mine = pl.ds(pl.multiple_of(me_d * own, own), own)
         count = counts_ref[:, mine]
         w_re = [jnp.zeros((group, own), jnp.float32) for _ in range(groups)]
         w_im = [jnp.zeros((group, own), jnp.float32) for _ in range(groups)]
@@ -109,7 +118,6 @@
 
         for copy in v_copies:
             copy.wait()
-        total = vt_ref[:, pl.ds(pl.multiple_of(me_d * own, own), own)]
         for k in range(n_dof - 1):
             total = total + recv_v[k].astype(jnp.float32)
         v_re = total[0:wave_count]
@@ -151,7 +159,8 @@
         in_specs=[pl.BlockSpec(memory_space=pltpu.VMEM)] * 6,
         out_specs=pl.BlockSpec(memory_space=pltpu.VMEM),
         scratch_shapes=[
-            pltpu.VMEM((n_dof - 1, modes, own), vt_link.dtype),
+            pltpu.VMEM((modes, n_dof * own), jnp.bfloat16),
+            pltpu.VMEM((n_dof - 1, modes, own), jnp.bfloat16),
             pltpu.VMEM((n_wave, pad, own), jnp.float32),
             pltpu.VMEM((n_wave - 1, pad, own), jnp.float32),
             pltpu.SemaphoreType.DMA((n_dof - 1,)),
@@ -160,7 +169,7 @@
             pltpu.SemaphoreType.DMA((n_wave - 1,)),
         ],
         compiler_params=pltpu.CompilerParams(collective_id=0, has_side_effects=True),
-    )(vt, vt_link, rows_t, counts_row, pos_t, load_t)
+    )(h_cat, coupling, rows_t, counts_row, pos_t, load_t)
 
 
 def body(green, rough, axle_pos, axle_load, rows, counts, coupling):
@@ -182,11 +191,7 @@
     gim_rim = prod[1, :, 2] + prod[1, :, 3]
     h_cat = jnp.concatenate([gre_rre - gim_rim, gre_rim + gim_rre], axis=0)
 
-    vt_part = lax.dot_general(
-        h_cat, coupling, (((1,), (1,)), ((), ())),
-        precision=lax.Precision.HIGHEST, preferred_element_type=jnp.float32,
-    )
-    return exchange(vt_part, vt_part.astype(jnp.bfloat16), rows.T, counts.reshape(1, -1), axle_pos.T, axle_load.T, wave_count).T
+    return exchange(h_cat, coupling, rows.T, counts.reshape(1, -1), axle_pos.T, axle_load.T, wave_count).T
 
 
 def solution(mesh):

time: 33.2 us -> 32.2 us (0.970)
  matrix products: 8.39 us -> 7.12 us
  other arithmetic: 0.44 us -> 0.91 us
    dot_general x1 -> x0, matrix products: 1.27 us -> none  [body(): lax.dot_general(h_cat, coupling, (((1,), (1,)), ((), ())), precision=lax....]
    concatenate x0 -> x1, other arithmetic: none -> 0.62 us  [body(): h_cat = jnp.concatenate([gre_rre - gim_rim, gre_rim + gim_rre], axis=0)]
    unnamed x3 -> x1, local copies, waits for them, and re-layouts: 1.28 us -> 1.26 us
where the time goes in v10:
time: 32.2 us; the launch traced here: 32 us
  Pallas kernels  21.3 us (66%)
  matrix products  7.12 us (22%)
  local copies, waits for them, and re-layouts  2.57 us (8%)
  other arithmetic  0.91 us (3%)
    pallas_call x1, Pallas kernels, exchange(): pl.pallas_call(kernel, out_shape=jax.ShapeDtypeStruct((per_wave, own), jn...  21.3 us
    dot_general x1, matrix products, body(): jnp.einsum('mkj,gmji->gmki', lhs, green, preferred_element_type=jnp.float32)  7.12 us
    unnamed x1, local copies, waits for them, and re-layouts  1.26 us
    slice x1, local copies, waits for them, and re-layouts, body(): re_hi, re_lo = split_bf16(rough[0])  0.99 us

profile of v10, /device:TPU:1, one launch (start us, length us, event | category | flops | bytes accessed | tf_op | source)
XLA Modules:
  0.0 32.0 jit_solution(12248452839054933285)
XLA Ops:
  0.0 1.0 %fusion.15 = (f32[1,64,512]{2,1,0:T(8,128)S(1)}, f32[1,64,512]{2,1,0:T(8,128)S(1)}) fusion(f32[2,64,512]{2,1,0:T(8,128)} %param.8), kind=kLoop, calls=%fused_computation.26 | loop fusion | bytes 524288 | tf_op jit(solution)/shard_map/slice | solution.py:184
  1.0 0.3 subtract_convert_fusion
  1.3 0.3 fusion.8
  1.5 7.1 %fusion = f32[64,4,2,128]{3,1,2,0:T(4,128)S(1)} fusion(bf16[2,64,512,128]{3,2,1,0:T(8,128)(2,1)} %param.7, bf16[64,1,512]{2,1,0:T(2,128)(2,1)S(1)} %get-tuple-element.9, bf16[64,1,512]{2,1,0:T(2,128)(2,1)S(1)} %get-tuple-element.12, bf16[64,1,512]{2,1,0:T(2,128)(2,1)S(1)} %get-tuple-element.10, bf16[64,1,512]{2,1,0:T(2,128)(2,1)S(1)} %get-tuple-element.11), kind=kOutput, calls=%fused_computation | convolution fusion | flops 68157440 | bytes 17301504 | tf_op jit(solution)/shard_map/mkj,gmji->gmki/dot_general | solution.py:187
  8.7 0.1 copy.32
  8.8 0.6 %pad_maximum_fusion.h_ref = f32[128,128]{1,0:T(8,128)} fusion(f32[64,128]{1,0:T(8,128)S(1)} %get-tuple-element.6, f32[64,128]{1,0:T(8,128)S(1)} %get-tuple-element.5), kind=kLoop, calls=%fused_computation.16 | loop fusion | flops 16384 | bytes 131072 | tf_op jit(solution)/shard_map/concatenate | solution.py:192
  9.4 21.3 %shard_map.73 = f32[4,256]{1,0:T(4,128)} custom-call(f32[128,128]{1,0:T(8,128)} %pad_maximum_fusion.h_ref, bf16[1024,128]{1,0:T(8,128)(2,1)} %cpl_ref.1, s32[16,1024]{1,0:T(8,128)} %bitcast.34, s32[1,1024]{1,0:T(1,128)} %bitcast.38, s32[32,128]{1,0:T(8,128)} %bitcast.36, f32[32,128]{1,0:T(8,128)} %bitcast.37), custom_call_target="tpu_custom_call" | custom-call | tf_op jit(solution)/shard_map/pallas_call | solution.py:156
  30.7 1.3 %copy.34 = f32[256,4]{0,1:T(4,128)} copy(f32[256,4]{0,1:T(4,128)} %bitcast.35) | data formatting | bytes 8192
  (1 shorter events, 0.0 us)

commit v11 on v10

--- a/solution.py
+++ b/solution.py
@@ -181,14 +181,13 @@
     wave_size = lax.axis_size("wave")
     own_buildings = building_count // dof_size
 
-    re_hi, re_lo = split_bf16(rough[0])
-    im_hi, im_lo = split_bf16(rough[1])
-    lhs = jnp.stack([re_hi, re_lo, im_hi, im_lo], axis=1)
-    prod = jnp.einsum("mkj,gmji->gmki", lhs, green, preferred_element_type=jnp.float32)
-    gre_rre = prod[0, :, 0] + prod[0, :, 1]
-    gre_rim = prod[0, :, 2] + prod[0, :, 3]
-    gim_rre = prod[1, :, 0] + prod[1, :, 1]
-    gim_rim = prod[1, :, 2] + prod[1, :, 3]
+    lhs = jnp.transpose(rough, (1, 0, 2))
+    prod = jnp.einsum("mkj,gmji->gmki", lhs, green.astype(jnp.float32),
+                      precision=lax.Precision.HIGH, preferred_element_type=jnp.float32)
+    gre_rre = prod[0, :, 0]
+    gre_rim = prod[0, :, 1]
+    gim_rre = prod[1, :, 0]
+    gim_rim = prod[1, :, 1]
     h_cat = jnp.concatenate([gre_rre - gim_rim, gre_rim + gim_rre], axis=0)
 
     return exchange(h_cat, coupling, rows.T, counts.reshape(1, -1), axle_pos.T, axle_load.T, wave_count).T

time: 32.2 us -> 32.5 us (level)
  matrix products: 7.12 us -> 8.09 us
  local copies, waits for them, and re-layouts: 2.57 us -> 2.24 us
    slice x1 -> x0, local copies, waits for them, and re-layouts: 0.99 us -> none  [body(): re_hi, re_lo = split_bf16(rough[0])]
    dot_general x1, matrix products: 7.12 us -> 8.09 us  [body(): jnp.einsum('mkj,gmji->gmki', lhs, green.astype(jnp.float32), precision=la...]
    unnamed x1 -> x3, local copies, waits for them, and re-layouts: 1.26 us -> 2.23 us
where the time goes in v11:
time: 32.5 us; the launch traced here: 32.3 us
  Pallas kernels  21.3 us (66%)
  matrix products  8.09 us (25%)
  local copies, waits for them, and re-layouts  2.24 us (7%)
  other arithmetic  0.63 us (2%)
    pallas_call x1, Pallas kernels, exchange(): pl.pallas_call(kernel, out_shape=jax.ShapeDtypeStruct((per_wave, own), jn...  21.3 us
    dot_general x1, matrix products, body(): jnp.einsum('mkj,gmji->gmki', lhs, green.astype(jnp.float32), precision=la...  8.09 us
    unnamed x3, local copies, waits for them, and re-layouts  2.23 us

profile of v11, /device:TPU:1, one launch (start us, length us, event | category | flops | bytes accessed | tf_op | source)
XLA Modules:
  0.0 32.3 jit_solution(11428051602256331460)
XLA Ops:
  0.0 0.0 copy-start
  0.0 0.9 %copy-done = f32[2,64,512]{2,1,0:T(8,128)S(1)} copy-done((f32[2,64,512]{2,1,0:T(8,128)S(1)}, f32[2,64,512]{2,1,0:T(8,128)}, u32[]{:S(2)}) %copy-start) | copy-done | bytes 262168
  1.0 8.1 %fusion = f32[64,2,128,2]{2,3,1,0:T(2,128)S(1)} fusion(bf16[2,64,512,128]{3,2,1,0:T(8,128)(2,1)} %param.7, f32[64,2,512,1]{2,0,1,3:T(8,128)S(1)} %bitcast.15), kind=kOutput, calls=%fused_computation | convolution fusion | flops 100663296 | bytes 17170432 | tf_op jit(solution)/shard_map/mkj,gmji->gmki/dot_general | solution.py:185
  9.1 0.6 %pad_maximum_fusion.h_ref = f32[128,128]{1,0:T(8,128)} fusion(f32[64,128]{1,0:T(8,128)S(1)} %get-tuple-element.6, f32[64,128]{1,0:T(8,128)S(1)} %get-tuple-element.5), kind=kLoop, calls=%fused_computation.4 | loop fusion | flops 16384 | bytes 131072 | tf_op jit(solution)/shard_map/concatenate | solution.py:191
  9.7 21.3 %shard_map.73 = f32[4,256]{1,0:T(4,128)} custom-call(f32[128,128]{1,0:T(8,128)} %pad_maximum_fusion.h_ref, bf16[1024,128]{1,0:T(8,128)(2,1)} %cpl_ref.1, s32[16,1024]{1,0:T(8,128)} %bitcast.17, s32[1,1024]{1,0:T(1,128)} %bitcast.21, s32[32,128]{1,0:T(8,128)} %bitcast.19, f32[32,128]{1,0:T(8,128)} %bitcast.20), custom_call_target="tpu_custom_call" | custom-call | tf_op jit(solution)/shard_map/pallas_call | solution.py:156
  31.1 1.3 %copy.21 = f32[256,4]{0,1:T(4,128)} copy(f32[256,4]{0,1:T(4,128)} %bitcast.18) | data formatting | bytes 8192
  (2 shorter events, 0.0 us)
Async XLA Ops:
  0.0 1.0 %copy-start = (f32[2,64,512]{2,1,0:T(8,128)S(1)}, f32[2,64,512]{2,1,0:T(8,128)}, u32[]{:S(2)}) copy-start(f32[2,64,512]{2,1,0:T(8,128)} %param.8) | copy-start | bytes 786436

commit v12 on v11

--- a/solution.py
+++ b/solution.py
@@ -181,8 +181,7 @@
     wave_size = lax.axis_size("wave")
     own_buildings = building_count // dof_size
 
-    lhs = jnp.transpose(rough, (1, 0, 2))
-    prod = jnp.einsum("mkj,gmji->gmki", lhs, green.astype(jnp.float32),
+    prod = jnp.einsum("kmj,gmji->gmki", rough, green.astype(jnp.float32),
                       precision=lax.Precision.HIGH, preferred_element_type=jnp.float32)
     gre_rre = prod[0, :, 0]
     gre_rim = prod[0, :, 1]

time: 32.5 us -> 32.5 us (level)
  no operation moved by 1% of the time
where the time goes in v12:
time: 32.5 us; the launch traced here: 32.3 us
  Pallas kernels  21.3 us (66%)
  matrix products  8.09 us (25%)
  local copies, waits for them, and re-layouts  2.24 us (7%)
  other arithmetic  0.63 us (2%)
    pallas_call x1, Pallas kernels, exchange(): pl.pallas_call(kernel, out_shape=jax.ShapeDtypeStruct((per_wave, own), jn...  21.3 us
    dot_general x1, matrix products, body(): jnp.einsum('kmj,gmji->gmki', rough, green.astype(jnp.float32), precision=...  8.09 us
    unnamed x3, local copies, waits for them, and re-layouts  2.23 us

profile of v12, /device:TPU:1, one launch (start us, length us, event | category | flops | bytes accessed | tf_op | source)
XLA Modules:
  0.0 32.3 jit_solution(11428051602256331460)
XLA Ops:
  0.0 0.0 copy-start
  0.0 0.9 %copy-done = f32[2,64,512]{2,1,0:T(8,128)S(1)} copy-done((f32[2,64,512]{2,1,0:T(8,128)S(1)}, f32[2,64,512]{2,1,0:T(8,128)}, u32[]{:S(2)}) %copy-start) | copy-done | bytes 262168
  1.0 8.1 %fusion = f32[64,2,128,2]{2,3,1,0:T(2,128)S(1)} fusion(bf16[2,64,512,128]{3,2,1,0:T(8,128)(2,1)} %param.7, f32[2,64,512,1]{2,1,0,3:T(8,128)S(1)} %bitcast.13), kind=kOutput, calls=%fused_computation | convolution fusion | flops 100663296 | bytes 17170432 | tf_op jit(solution)/shard_map/kmj,gmji->gmki/dot_general | solution.py:184
  9.1 0.6 %pad_maximum_fusion.h_ref = f32[128,128]{1,0:T(8,128)} fusion(f32[64,128]{1,0:T(8,128)S(1)} %get-tuple-element.6, f32[64,128]{1,0:T(8,128)S(1)} %get-tuple-element.5), kind=kLoop, calls=%fused_computation.4 | loop fusion | flops 16384 | bytes 131072 | tf_op jit(solution)/shard_map/concatenate | solution.py:190
  9.7 21.3 %shard_map.73 = f32[4,256]{1,0:T(4,128)} custom-call(f32[128,128]{1,0:T(8,128)} %pad_maximum_fusion.h_ref, bf16[1024,128]{1,0:T(8,128)(2,1)} %cpl_ref.1, s32[16,1024]{1,0:T(8,128)} %bitcast.15, s32[1,1024]{1,0:T(1,128)} %bitcast.19, s32[32,128]{1,0:T(8,128)} %bitcast.17, f32[32,128]{1,0:T(8,128)} %bitcast.18), custom_call_target="tpu_custom_call" | custom-call | tf_op jit(solution)/shard_map/pallas_call | solution.py:156
  31.1 1.3 %copy.21 = f32[256,4]{0,1:T(4,128)} copy(f32[256,4]{0,1:T(4,128)} %bitcast.16) | data formatting | bytes 8192
  (2 shorter events, 0.0 us)
Async XLA Ops:
  0.0 1.0 %copy-start = (f32[2,64,512]{2,1,0:T(8,128)S(1)}, f32[2,64,512]{2,1,0:T(8,128)}, u32[]{:S(2)}) copy-start(f32[2,64,512]{2,1,0:T(8,128)} %param.8) | copy-start | bytes 786436
